TPU v7x, 32 devices: a whole 2x2x4 slice. The times are simulated.
32 devices in a mesh: twin: 2 (over y), gx: 4 (over z), gy: 2 (over core), gz: 2 (over x).
Axes of the slice: x: 2, y: 2, z: 4, core: 2. Of those that a mesh axis runs over, the one named last changes fastest.
Arguments:
- potential: float32 [64, 32, 256], P(('twin', 'gx'), 'gy', 'gz'), parts along dimension 0, may hold values from 0 to 1
- gating: float32 [64, 32, 256], P(('twin', 'gx'), 'gy', 'gz'), parts along dimension 0, may hold values from 0 to 1
- adjoint_v: float32 [64, 32, 256], P(('twin', 'gx'), 'gy', 'gz'), parts along dimension 0, may hold values from -6 to 6
- adjoint_h: float32 [64, 32, 256], P(('twin', 'gx'), 'gy', 'gz'), parts along dimension 0, may hold values from -6 to 6
- recorded: float32 [64, 32, 256], P(('twin', 'gx'), 'gy', 'gz'), parts along dimension 0, may hold values from 0 to 1
- tissue_mask: int32 [64, 32, 256], P(('twin', 'gx'), 'gy', 'gz'), parts along dimension 0, may hold values from 0 to 1
- fibre_sector: int32 [64, 32, 256], P(('twin', 'gx'), 'gy', 'gz'), parts along dimension 0, may hold values from 0 to 11
- region_label: int32 [64, 32, 256], P(('twin', 'gx'), 'gy', 'gz'), parts along dimension 0, may hold values from 0 to 15
- fibre_table: float32 [24, 9], P('twin'), parts along dimension 0, may hold values from 0.005 to 0.025
- conductance: float32 [32], P('twin'), parts along dimension 0, may hold values from 0.5 to 2
Outputs:
- lambda_v: float32 [64, 32, 256], P(('twin', 'gx'), 'gy', 'gz'), parts along dimension 0
- lambda_h: float32 [64, 32, 256], P(('twin', 'gx'), 'gy', 'gz'), parts along dimension 0
- sensitivity: float32 [32], P('twin'), parts along dimension 0
There are 2 independent parts, one for each index of `twin`. A program takes and returns all parts, laid end to end along the dimension named above; each array names one. Nothing has to cross between parts.
All inputs are finite; a program needn't handle non-finite values.
Results may differ from a plain program's by a relative error of at most 0.0003.
Values sent between devices are 32-bit elements; how exact they have to be, the bound alone decides.
No kernel may reach another device: no remote copies, remote signals or barrier semaphores. Data moves between devices by JAX's collectives and lax.ppermute only.
A program may use at most 64 MiB of HBM per device.

v0:
```python
import math
import jax
import jax.numpy as jnp
from jax import lax
from jax.sharding import PartitionSpec as P

WINDOW_STEPS = 3
step_size = 0.1
tau_inward = 0.3
tau_outward = 6.0
tau_opening = 12.0
tau_closing = 15.0
gate_level = 0.13
gate_width = 0.02
gradient_gain = 30.0
PAIR_OFFSETS = (
    (1, 0, 0),
    (0, 1, 0),
    (0, 0, 1),
    (1, 1, 0),
    (1, -1, 0),
    (1, 0, 1),
    (1, 0, -1),
    (0, 1, 1),
    (0, 1, -1),
)


def extended(array, sides, width):
    for axis, dim in sides:
        count, length = (lax.axis_size(axis), array.shape[dim])
        up = [(i, (i + 1) % count) for i in range(count - 1)]
        down = [(j, i) for i, j in up]
        last = lax.slice_in_dim(array, length - width, length, axis=dim)
        initial = lax.slice_in_dim(array, 0, width, axis=dim)
        before = lax.ppermute(last, axis, up)
        after = lax.ppermute(initial, axis, down)
        array = jnp.concatenate([before, array, after], axis=dim)
    return array


def crop(array, trim):
    if trim == 0:
        return array
    return array[..., trim:-trim, trim:-trim, trim:-trim]


def shifted(padded, offset):
    sizes = [padded.shape[-3 + axis] - 2 for axis in range(3)]
    starts = [1 + offset[axis] for axis in range(3)]
    return padded[
        ...,
        starts[0] : starts[0] + sizes[0],
        starts[1] : starts[1] + sizes[1],
        starts[2] : starts[2] + sizes[2],
    ]


def neighbour_terms(field_pad, tissue_pad, flux_pad):
    centre = crop(field_pad, 1)
    tissue_mid = crop(tissue_pad, 1)
    flux_mid = crop(flux_pad, 1)
    total = jnp.zeros_like(centre)
    for direction, base in enumerate(PAIR_OFFSETS):
        for sign in (1, -1):
            offset = tuple((sign * part for part in base))
            coupling = 0.5 * (
                flux_mid[direction] * shifted(tissue_pad, offset)
                + shifted(flux_pad[direction], offset) * tissue_mid
            )
            total = total + coupling * (shifted(field_pad, offset) - centre)
    return total


def region_terms(adjoint_pad, field_pad, tissue_pad, fibre_mid):
    adjoint_mid = crop(adjoint_pad, 1)
    centre = crop(field_pad, 1)
    total = jnp.zeros_like(centre)
    for direction, base in enumerate(PAIR_OFFSETS):
        for sign in (1, -1):
            offset = tuple((sign * part for part in base))
            weight = shifted(tissue_pad, offset) * fibre_mid[direction]
            total = total + weight * (shifted(adjoint_pad, offset) - adjoint_mid) * (
                shifted(field_pad, offset) - centre
            )
    return -0.5 * crop(tissue_pad, 1) * total


def ionic(volts, gate_now):
    switch = jax.nn.sigmoid((volts - gate_level) / gate_width)
    drive_v = gate_now * volts * volts * (1.0 - volts) / tau_inward - volts / tau_outward
    drive_h = (1.0 - switch) * (1.0 - gate_now) / tau_opening - switch * gate_now / tau_closing
    return (drive_v, drive_h)


def ionic_partials(volts, gate_now):
    switch = jax.nn.sigmoid((volts - gate_level) / gate_width)
    slope = switch * (1.0 - switch) / gate_width
    deriv_vv = gate_now * (2.0 * volts - 3.0 * volts * volts) / tau_inward - 1.0 / tau_outward
    deriv_vh = volts * volts * (1.0 - volts) / tau_inward
    deriv_hv = slope * (-(1.0 - gate_now) / tau_opening - gate_now / tau_closing)
    deriv_hh = -(1.0 - switch) / tau_opening - switch / tau_closing
    return (deriv_vv, deriv_vh, deriv_hv, deriv_hh)


def forward_step(volts_pad, gate_now, tissue_mid, tissue_pad, flux_pad):
    volts = crop(volts_pad, 1)
    drive_v, drive_h = ionic(volts, gate_now)
    spread = neighbour_terms(volts_pad, tissue_pad, flux_pad)
    return (
        volts + tissue_mid * (spread + step_size * drive_v),
        gate_now + tissue_mid * step_size * drive_h,
    )


def local_coefficients(tissue_mask, fibre_sector, region_label, fibre_table, conductance):
    tissue_local = tissue_mask.astype(jnp.float32)
    local_factor = jnp.zeros(tissue_local.shape, jnp.float32)
    for label in range(conductance.shape[0]):
        local_factor = local_factor + jnp.where(region_label == label, conductance[label], 0.0)
    fibre_local = jnp.zeros((9,) + tissue_local.shape, jnp.float32)
    for label in range(fibre_table.shape[0]):
        fibre_local = fibre_local + jnp.where(
            (fibre_sector == label)[None], fibre_table[label][:, None, None, None], 0.0
        )
    flux_local = (tissue_local * local_factor)[None] * fibre_local
    return (tissue_local, fibre_local, flux_local)


def local(
    potential,
    gating,
    adjoint_v,
    adjoint_h,
    recorded,
    tissue_mask,
    fibre_sector,
    region_label,
    fibre_table,
    conductance,
):
    span = 1
    tissue_local, fibre_mid, flux_local = local_coefficients(
        tissue_mask, fibre_sector, region_label, fibre_table, conductance
    )
    flux_all = extended(flux_local, (("gx", 1), ("gy", 2), ("gz", 3)), span)
    tissue_all = jnp.where(flux_all[0] > 0.0, 1.0, 0.0).astype(jnp.float32)
    tissue_pad = crop(tissue_all, span - 1)
    flux_pad = crop(flux_all, span - 1)
    saved_pads = []
    saved_gates = []
    volts = potential
    gate_now = gating
    for step in range(WINDOW_STEPS):
        volts_pad = extended(volts, (("gx", 0), ("gy", 1), ("gz", 2)), 1)
        saved_pads.append(volts_pad)
        saved_gates.append(gate_now)
        volts, gate_now = forward_step(volts_pad, gate_now, tissue_local, tissue_pad, flux_pad)
    back_v = adjoint_v + tissue_local * (volts - recorded)
    back_h = adjoint_h
    region_count = conductance.shape[0]
    selector = (
        region_label[None] == jnp.arange(region_count, dtype=jnp.int32)[:, None, None, None]
    ).astype(jnp.float32)
    total = jnp.zeros((region_count,), jnp.float32)
    for step in reversed(range(WINDOW_STEPS)):
        masked = tissue_local * back_v
        masked_pad = extended(masked, (("gx", 0), ("gy", 1), ("gz", 2)), 1)
        volts_pad = saved_pads[step]
        terms = region_terms(masked_pad, volts_pad, tissue_pad, fibre_mid)
        partial_sums = jnp.einsum(
            "rxyz,xyz->r", selector, terms, precision=jax.lax.Precision.HIGHEST
        )
        total = total + lax.psum(partial_sums, ("gx", "gy", "gz"))
        deriv_vv, deriv_vh, deriv_hv, deriv_hh = ionic_partials(
            crop(volts_pad, 1), saved_gates[step]
        )
        spread = neighbour_terms(masked_pad, tissue_pad, flux_pad)
        next_v = (
            back_v + spread + step_size * tissue_local * (deriv_vv * back_v + deriv_hv * back_h)
        )
        next_h = back_h + step_size * tissue_local * (deriv_vh * back_v + deriv_hh * back_h)
        back_v, back_h = (next_v, next_h)
    cells = (
        potential.shape[0]
        * potential.shape[1]
        * potential.shape[2]
        * lax.axis_size("gx")
        * lax.axis_size("gy")
        * lax.axis_size("gz")
    )
    scale = gradient_gain / math.sqrt(cells / region_count)
    return (back_v, back_h, total * scale)


def solution(mesh):
    in_specs = (
        P(("twin", "gx"), "gy", "gz"),
        P(("twin", "gx"), "gy", "gz"),
        P(("twin", "gx"), "gy", "gz"),
        P(("twin", "gx"), "gy", "gz"),
        P(("twin", "gx"), "gy", "gz"),
        P(("twin", "gx"), "gy", "gz"),
        P(("twin", "gx"), "gy", "gz"),
        P(("twin", "gx"), "gy", "gz"),
        P("twin", None),
        P("twin"),
    )
    out_specs = (P(("twin", "gx"), "gy", "gz"), P(("twin", "gx"), "gy", "gz"), P("twin"))
    return jax.shard_map(local, mesh=mesh, in_specs=in_specs, out_specs=out_specs, check_vma=False)
```

profile of v0, /device:TPU:0, one launch (start us, length us, event | category | flops | bytes accessed | tf_op | source)
XLA Modules:
  0.0 217.4 jit_solution(543356595917093015)
XLA Ops:
  1.4 4.9 %collective-permute-start.7 = (f32[1,16,128]{2,1,0:T(8,128)S(1)}, f32[1,16,128]{2,1,0:T(8,128)S(1)}, u32[]{:S(2)}, u32[]{:S(2)}) collective-permute-start(f32[1,16,128]{2,1,0:T(8,128)S(1)} %get-tuple-element.115), channel_id=1, source_target_pairs={{0,4},{4,8},{8,12},{1,5},{5,9},{9,13},{2,6},{6,10},{10,14},{3,7},{... | collective-permute-start | bytes 24584 | tf_op jit(solution)/shard_map/ppermute | solution.py:36
  6.4 1.3 collective-permute-start.6
  8.7 2.0 fusion.198
  11.6 11.1 %add_multiply_fusion.3 = f32[8,16,128]{2,1,0:T(8,128)S(1)} fusion(s32[8,16,128]{2,1,0:T(8,128)} %param.15, s32[8,16,128]{2,1,0:T(8,128)} %param.17, f32[]{:T(128)} %bitcast.15, f32[]{:T(128)} %bitcast.14, f32[]{:T(128)} %bitcast.13, f32[]{:T(128)} %bitcast.12, f32[]{:T(128)} %bitcast.11, f32[]{:T(128)} %bitcast.10, f32[]{:T(128)} %bitcast.9, f32[]{:T(128)} %bitcast.8, ...), kind=kLoop, calls=%fused_computation.360 | loop fusion | flops 802816 | bytes 196672 | tf_op jit(solution)/shard_map/mul | solution.py:126
  23.8 1.5 collective-permute-start.9
  26.6 4.4 %collective-permute-start = (f32[9,1,16,128]{3,2,1,0:T(8,128)S(1)}, f32[9,1,16,128]{3,2,1,0:T(8,128)S(1)}, u32[]{:S(2)}, u32[]{:S(2)}) collective-permute-start(f32[9,1,16,128]{3,2,1,0:T(8,128)S(1)} %get-tuple-element.45), channel_id=1, source_target_pairs={{0,4},{4,8},{8,12},{1,5},{5,9},{9,13},{2,6},{6,10},{10,14},{3,7},{... | collective-permute-start | bytes 221192 | tf_op jit(solution)/shard_map/ppermute | solution.py:36
  33.5 4.4 %collective-permute-done.1 = f32[9,1,16,128]{3,2,1,0:T(8,128)S(1)} collective-permute-done((f32[9,1,16,128]{3,2,1,0:T(8,128)S(1)}, f32[9,1,16,128]{3,2,1,0:T(8,128)S(1)}, u32[]{:S(2)}, u32[]{:S(2)}) %collective-permute-start.1) | collective-permute-done | bytes 73760 | tf_op jit(solution)/shard_map/ppermute | solution.py:37
  37.9 1.9 collective-permute-start.2
  41.2 3.4 %collective-permute-start.11 = (f32[10,18,1]{2,1,0:T(8,128)S(1)}, f32[10,18,1]{2,1,0:T(8,128)S(1)}, u32[]{:S(2)}, u32[]{:S(2)}) collective-permute-start(f32[10,18,1]{2,1,0:T(8,128)S(1)} %get-tuple-element.57), channel_id=1, source_target_pairs={{0,1},{2,3},{4,5},{6,7},{8,9},{10,11},{12,13},{14,15},{16,17},{18,... | collective-permute-start | bytes 2168 | tf_op jit(solution)/shard_map/ppermute | solution.py:36
  46.2 1.4 fusion.183
  47.5 2.5 %copy.166 = f32[9,10,18,1]{2,3,1,0:T(1,128)} copy(f32[9,10,18,1]{3,2,1,0:T(8,128)} %get-tuple-element.41) | data formatting | bytes 12960
  51.9 5.8 %collective-permute-start.4 = (f32[9,10,18,1]{2,3,1,0:T(1,128)}, f32[9,10,18,1]{2,3,1,0:T(1,128)}, u32[]{:S(2)}, u32[]{:S(2)}) collective-permute-start(f32[9,10,18,1]{2,3,1,0:T(1,128)} %copy.166), channel_id=1, source_target_pairs={{0,1},{2,3},{4,5},{6,7},{8,9},{10,11},{12,13},{14,15},{16,17},{18,... | collective-permute-start | bytes 19448 | tf_op jit(solution)/shard_map/ppermute | solution.py:36
  59.1 1.4 copy.157
  60.6 2.4 %copy.158 = f32[9,10,18,1]{3,2,1,0:T(8,128)} copy(f32[9,10,18,1]{2,3,1,0:T(1,128)} %collective-permute-done.5) | data formatting | bytes 12960 | tf_op jit(solution)/shard_map/ppermute | solution.py:37
  63.0 2.6 %pad_maximum_fusion = f32[9,10,18,130]{3,2,1,0:T(8,128)S(1)} fusion(f32[9,10,18,1]{3,2,1,0:T(8,128)} %copy.158, f32[9,10,1,128]{3,2,1,0:T(1,128)S(1)} %collective-permute-done.3, f32[9,1,16,128]{3,2,1,0:T(8,128)S(1)} %collective-permute-done.1, f32[9,8,16,128]{3,2,1,0:T(8,128)S(1)} %get-tuple-element.30, f32[9,1,16,128]{3,2,1,0:T(8,128)S(1)} %collective-permute-done, ...), kind=kLoop, calls=%fused_computation | loop fusion | flops 1263600 | bytes 1684800 | tf_op jit(solution)/shard_map/concatenate | solution.py:38
  67.4 3.5 %collective-permute-start.13 = (f32[1,16,128]{2,1,0:T(8,128)S(1)}, f32[1,16,128]{2,1,0:T(8,128)S(1)}, u32[]{:S(2)}, u32[]{:S(2)}) collective-permute-start(f32[1,16,128]{2,1,0:T(8,128)S(1)} %get-tuple-element.101), channel_id=1, source_target_pairs={{0,4},{4,8},{8,12},{1,5},{5,9},{9,13},{2,6},{6,10},{10,14},{3,7},{... | collective-permute-start | bytes 24584 | tf_op jit(solution)/shard_map/ppermute | solution.py:36
  72.3 4.2 %collective-permute-done.12 = f32[1,16,128]{2,1,0:T(8,128)S(1)} collective-permute-done((f32[1,16,128]{2,1,0:T(8,128)S(1)}, f32[1,16,128]{2,1,0:T(8,128)S(1)}, u32[]{:S(2)}, u32[]{:S(2)}) %collective-permute-start.12) | collective-permute-done | bytes 8224 | tf_op jit(solution)/shard_map/ppermute | solution.py:37
  79.1 1.8 collective-permute-done.14
  81.0 4.3 %collective-permute-start.17 = (f32[10,18,1]{2,1,0:T(8,128)S(1)}, f32[10,18,1]{2,1,0:T(8,128)S(1)}, u32[]{:S(2)}, u32[]{:S(2)}) collective-permute-start(f32[10,18,1]{2,1,0:T(8,128)S(1)} %get-tuple-element.55), channel_id=1, source_target_pairs={{0,1},{2,3},{4,5},{6,7},{8,9},{10,11},{12,13},{14,15},{16,17},{18,... | collective-permute-start | bytes 2168 | tf_op jit(solution)/shard_map/ppermute | solution.py:36
  86.6 1.6 collective-permute-done.17
  88.2 4.1 %collective-permute-done.16 = f32[10,18,1]{2,1,0:T(8,128)S(1)} collective-permute-done((f32[10,18,1]{2,1,0:T(8,128)S(1)}, f32[10,18,1]{2,1,0:T(8,128)S(1)}, u32[]{:S(2)}, u32[]{:S(2)}) %collective-permute-start.16) | collective-permute-done | bytes 752 | tf_op jit(solution)/shard_map/ppermute | solution.py:37
  92.8 3.6 %collective-permute-start.19 = (f32[1,16,128]{2,1,0:T(8,128)S(1)}, f32[1,16,128]{2,1,0:T(8,128)S(1)}, u32[]{:S(2)}, u32[]{:S(2)}) collective-permute-start(f32[1,16,128]{2,1,0:T(8,128)S(1)} %get-tuple-element.99), channel_id=1, source_target_pairs={{0,4},{4,8},{8,12},{1,5},{5,9},{9,13},{2,6},{6,10},{10,14},{3,7},{... | collective-permute-start | bytes 24584 | tf_op jit(solution)/shard_map/ppermute | solution.py:36
  97.8 4.2 %collective-permute-done.18 = f32[1,16,128]{2,1,0:T(8,128)S(1)} collective-permute-done((f32[1,16,128]{2,1,0:T(8,128)S(1)}, f32[1,16,128]{2,1,0:T(8,128)S(1)}, u32[]{:S(2)}, u32[]{:S(2)}) %collective-permute-start.18) | collective-permute-done | bytes 8224 | tf_op jit(solution)/shard_map/ppermute | solution.py:37
  104.6 1.8 collective-permute-done.20
  106.5 1.5 collective-permute-start.23
  109.3 1.7 collective-permute-done.23
  111.0 4.1 %collective-permute-done.22 = f32[10,18,1]{2,1,0:T(8,128)S(1)} collective-permute-done((f32[10,18,1]{2,1,0:T(8,128)S(1)}, f32[10,18,1]{2,1,0:T(8,128)S(1)}, u32[]{:S(2)}, u32[]{:S(2)}) %collective-permute-start.22) | collective-permute-done | bytes 752 | tf_op jit(solution)/shard_map/ppermute | solution.py:37
  115.9 1.9 collective-permute-start.25
  119.2 4.2 %collective-permute-done.24 = f32[1,16,128]{2,1,0:T(8,128)S(1)} collective-permute-done((f32[1,16,128]{2,1,0:T(8,128)S(1)}, f32[1,16,128]{2,1,0:T(8,128)S(1)}, u32[]{:S(2)}, u32[]{:S(2)}) %collective-permute-start.24) | collective-permute-done | bytes 8224 | tf_op jit(solution)/shard_map/ppermute | solution.py:37
  124.7 1.4 collective-permute-start.26
  126.3 1.6 collective-permute-done.26
  128.0 1.5 collective-permute-start.29
  130.8 1.7 collective-permute-done.29
  132.5 4.1 %collective-permute-done.28 = f32[10,18,1]{2,1,0:T(8,128)S(1)} collective-permute-done((f32[10,18,1]{2,1,0:T(8,128)S(1)}, f32[10,18,1]{2,1,0:T(8,128)S(1)}, u32[]{:S(2)}, u32[]{:S(2)}) %collective-permute-start.28) | collective-permute-done | bytes 752 | tf_op jit(solution)/shard_map/ppermute | solution.py:37
  137.4 1.9 collective-permute-start.31
  141.4 3.5 %collective-permute-done.30 = f32[1,16,128]{2,1,0:T(8,128)S(1)} collective-permute-done((f32[1,16,128]{2,1,0:T(8,128)S(1)}, f32[1,16,128]{2,1,0:T(8,128)S(1)}, u32[]{:S(2)}, u32[]{:S(2)}) %collective-permute-start.30) | collective-permute-done | bytes 8224 | tf_op jit(solution)/shard_map/ppermute | solution.py:37
  146.2 1.5 collective-permute-start.32
  149.4 1.5 collective-permute-start.35
  152.2 1.9 collective-permute-done.35
  154.0 4.1 %collective-permute-done.34 = f32[10,18,1]{2,1,0:T(8,128)S(1)} collective-permute-done((f32[10,18,1]{2,1,0:T(8,128)S(1)}, f32[10,18,1]{2,1,0:T(8,128)S(1)}, u32[]{:S(2)}, u32[]{:S(2)}) %collective-permute-start.34) | collective-permute-done | bytes 752 | tf_op jit(solution)/shard_map/ppermute | solution.py:37
  159.3 1.9 collective-permute-start.37
  163.1 3.6 %collective-permute-done.36 = f32[1,16,128]{2,1,0:T(8,128)S(1)} collective-permute-done((f32[1,16,128]{2,1,0:T(8,128)S(1)}, f32[1,16,128]{2,1,0:T(8,128)S(1)}, u32[]{:S(2)}, u32[]{:S(2)}) %collective-permute-start.36) | collective-permute-done | bytes 8224 | tf_op jit(solution)/shard_map/ppermute | solution.py:37
  171.2 1.5 collective-permute-start.41
  174.0 2.0 collective-permute-done.41
  176.0 4.1 %collective-permute-done.40 = f32[10,18,1]{2,1,0:T(8,128)S(1)} collective-permute-done((f32[10,18,1]{2,1,0:T(8,128)S(1)}, f32[10,18,1]{2,1,0:T(8,128)S(1)}, u32[]{:S(2)}, u32[]{:S(2)}) %collective-permute-start.40) | collective-permute-done | bytes 752 | tf_op jit(solution)/shard_map/ppermute | solution.py:37
  182.3 1.7 fusion.20
  183.9 29.5 %psum.25 = f32[16]{0:T(128)S(1)} all-reduce(f32[16]{0:T(128)S(1)} %fusion), channel_id=1, replica_groups=mesh['twin'=2,'gx'=4,'gy'=2,'gz'=2] {'gx','gy','gz'}, use_global_device_ids=true, to_apply=%region_0.1 | all-reduce | flops 16 | bytes 128 | tf_op jit(solution)/shard_map/psum | solution.py:174
  214.0 3.4 %fusion.14 = f32[8,16,128]{2,1,0:T(8,128)} fusion(f32[8,16,128]{2,1,0:T(8,128)} %param.11, f32[8,16,128]{2,1,0:T(8,128)S(1)} %copy-done.30, f32[8,16,128]{2,1,0:T(8,128)} %copy-done.16, f32[8,16,128]{2,1,0:T(8,128)} %copy-done.15, f32[8,16,128]{2,1,0:T(8,128)} %copy-done.14, f32[8,16,128]{2,1,0:T(8,128)} %copy-done.13, f32[8,16,128]{2,1,0:T(8,128)} %copy-done.12, ...), kind=kLoop, calls=%fused_computation.82 | loop fusion | flops 5701632 | bytes 6291456 | tf_op jit(solution)/shard_map/add | solution.py:180
  (218 shorter events, 49.7 us)
Async XLA Ops:
  1.4 22.3 %collective-permute-start.7 = (f32[1,16,128]{2,1,0:T(8,128)S(1)}, f32[1,16,128]{2,1,0:T(8,128)S(1)}, u32[]{:S(2)}, u32[]{:S(2)}) collective-permute-start(f32[1,16,128]{2,1,0:T(8,128)S(1)} %get-tuple-element.115), channel_id=1, source_target_pairs={{0,4},{4,8},{8,12},{1,5},{5,9},{9,13},{2,6},{6,10},{10,14},{3,7},{... | collective-permute-start | bytes 24584 | tf_op jit(solution)/shard_map/ppermute | solution.py:36
  6.4 17.4 %collective-permute-start.6 = (f32[1,16,128]{2,1,0:T(8,128)S(1)}, f32[1,16,128]{2,1,0:T(8,128)S(1)}, u32[]{:S(2)}, u32[]{:S(2)}) collective-permute-start(f32[1,16,128]{2,1,0:T(8,128)S(1)} %get-tuple-element.116), channel_id=1, source_target_pairs={{4,0},{8,4},{12,8},{5,1},{9,5},{13,9},{6,2},{10,6},{14,10},{7,3},{... | collective-permute-start | bytes 24584 | tf_op jit(solution)/shard_map/ppermute | solution.py:37
  23.8 8.5 %collective-permute-start.9 = (f32[10,1,128]{2,1,0:T(1,128)S(1)}, f32[10,1,128]{2,1,0:T(1,128)S(1)}, u32[]{:S(2)}, u32[]{:S(2)}) collective-permute-start(f32[10,1,128]{2,1,0:T(1,128)S(1)} %get-tuple-element.91), channel_id=1, source_target_pairs={{0,2},{1,3},{4,6},{5,7},{8,10},{9,11},{12,14},{13,15},{16,18},{17,... | collective-permute-start | bytes 15368 | tf_op jit(solution)/shard_map/ppermute | solution.py:36
  25.3 7.0 %collective-permute-start.8 = (f32[10,1,128]{2,1,0:T(1,128)S(1)}, f32[10,1,128]{2,1,0:T(1,128)S(1)}, u32[]{:S(2)}, u32[]{:S(2)}) collective-permute-start(f32[10,1,128]{2,1,0:T(1,128)S(1)} %get-tuple-element.92), channel_id=1, source_target_pairs={{2,0},{3,1},{6,4},{7,5},{10,8},{11,9},{14,12},{15,13},{18,16},{19,... | collective-permute-start | bytes 15368 | tf_op jit(solution)/shard_map/ppermute | solution.py:37
  26.6 6.9 %collective-permute-start = (f32[9,1,16,128]{3,2,1,0:T(8,128)S(1)}, f32[9,1,16,128]{3,2,1,0:T(8,128)S(1)}, u32[]{:S(2)}, u32[]{:S(2)}) collective-permute-start(f32[9,1,16,128]{3,2,1,0:T(8,128)S(1)} %get-tuple-element.45), channel_id=1, source_target_pairs={{0,4},{4,8},{8,12},{1,5},{5,9},{9,13},{2,6},{6,10},{10,14},{3,7},{... | collective-permute-start | bytes 221192 | tf_op jit(solution)/shard_map/ppermute | solution.py:36
  31.0 6.9 %collective-permute-start.1 = (f32[9,1,16,128]{3,2,1,0:T(8,128)S(1)}, f32[9,1,16,128]{3,2,1,0:T(8,128)S(1)}, u32[]{:S(2)}, u32[]{:S(2)}) collective-permute-start(f32[9,1,16,128]{3,2,1,0:T(8,128)S(1)} %get-tuple-element.46), channel_id=1, source_target_pairs={{4,0},{8,4},{12,8},{5,1},{9,5},{13,9},{6,2},{10,6},{14,10},{7,3},{... | collective-permute-start | bytes 221192 | tf_op jit(solution)/shard_map/ppermute | solution.py:37
  37.9 8.0 %collective-permute-start.2 = (f32[9,10,1,128]{3,2,1,0:T(1,128)S(1)}, f32[9,10,1,128]{3,2,1,0:T(1,128)S(1)}, u32[]{:S(2)}, u32[]{:S(2)}) collective-permute-start(f32[9,10,1,128]{3,2,1,0:T(1,128)S(1)} %get-tuple-element.43), channel_id=1, source_target_pairs={{0,2},{1,3},{4,6},{5,7},{8,10},{9,11},{12,14},{13,15},{16,18},{17,... | collective-permute-start | bytes 138248 | tf_op jit(solution)/shard_map/ppermute | solution.py:36
  39.8 6.1 %collective-permute-start.3 = (f32[9,10,1,128]{3,2,1,0:T(1,128)S(1)}, f32[9,10,1,128]{3,2,1,0:T(1,128)S(1)}, u32[]{:S(2)}, u32[]{:S(2)}) collective-permute-start(f32[9,10,1,128]{3,2,1,0:T(1,128)S(1)} %get-tuple-element.44), channel_id=1, source_target_pairs={{2,0},{3,1},{6,4},{7,5},{10,8},{11,9},{14,12},{15,13},{18,16},{19,... | collective-permute-start | bytes 138248 | tf_op jit(solution)/shard_map/ppermute | solution.py:37
  41.2 16.5 %collective-permute-start.11 = (f32[10,18,1]{2,1,0:T(8,128)S(1)}, f32[10,18,1]{2,1,0:T(8,128)S(1)}, u32[]{:S(2)}, u32[]{:S(2)}) collective-permute-start(f32[10,18,1]{2,1,0:T(8,128)S(1)} %get-tuple-element.57), channel_id=1, source_target_pairs={{0,1},{2,3},{4,5},{6,7},{8,9},{10,11},{12,13},{14,15},{16,17},{18,... | collective-permute-start | bytes 2168 | tf_op jit(solution)/shard_map/ppermute | solution.py:36
  44.6 13.1 %collective-permute-start.10 = (f32[10,18,1]{2,1,0:T(8,128)S(1)}, f32[10,18,1]{2,1,0:T(8,128)S(1)}, u32[]{:S(2)}, u32[]{:S(2)}) collective-permute-start(f32[10,18,1]{2,1,0:T(8,128)S(1)} %get-tuple-element.58), channel_id=1, source_target_pairs={{1,0},{3,2},{5,4},{7,6},{9,8},{11,10},{13,12},{15,14},{17,16},{19,... | collective-permute-start | bytes 2168 | tf_op jit(solution)/shard_map/ppermute | solution.py:37
  50.6 9.9 %collective-permute-start.5 = (f32[9,10,18,1]{2,3,1,0:T(1,128)S(1)}, f32[9,10,18,1]{2,3,1,0:T(1,128)}, u32[]{:S(2)}, u32[]{:S(2)}) collective-permute-start(f32[9,10,18,1]{2,3,1,0:T(1,128)S(1)} %copy.167), channel_id=1, source_target_pairs={{1,0},{3,2},{5,4},{7,6},{9,8},{11,10},{13,12},{15,14},{17,16},{19,... | collective-permute-start | bytes 19448 | tf_op jit(solution)/shard_map/ppermute | solution.py:37
  51.9 7.2 %collective-permute-start.4 = (f32[9,10,18,1]{2,3,1,0:T(1,128)}, f32[9,10,18,1]{2,3,1,0:T(1,128)}, u32[]{:S(2)}, u32[]{:S(2)}) collective-permute-start(f32[9,10,18,1]{2,3,1,0:T(1,128)} %copy.166), channel_id=1, source_target_pairs={{0,1},{2,3},{4,5},{6,7},{8,9},{10,11},{12,13},{14,15},{16,17},{18,... | collective-permute-start | bytes 19448 | tf_op jit(solution)/shard_map/ppermute | solution.py:36
  67.3 114.7 %copy-start.2 = (f32[8,16,128]{2,1,0:T(8,128)}, f32[8,16,128]{2,1,0:T(8,128)S(1)}, u32[]{:S(2)}) copy-start(f32[8,16,128]{2,1,0:T(8,128)S(1)} %get-tuple-element.15) | copy-start | bytes 196612
  67.3 114.7 %copy-start.3 = (f32[8,16,128]{2,1,0:T(8,128)}, f32[8,16,128]{2,1,0:T(8,128)S(1)}, u32[]{:S(2)}) copy-start(f32[8,16,128]{2,1,0:T(8,128)S(1)} %get-tuple-element.16) | copy-start | bytes 196612
  67.3 114.7 %copy-start.4 = (f32[8,16,128]{2,1,0:T(8,128)}, f32[8,16,128]{2,1,0:T(8,128)S(1)}, u32[]{:S(2)}) copy-start(f32[8,16,128]{2,1,0:T(8,128)S(1)} %get-tuple-element.17) | copy-start | bytes 196612
  67.3 114.7 %copy-start.5 = (f32[8,16,128]{2,1,0:T(8,128)}, f32[8,16,128]{2,1,0:T(8,128)S(1)}, u32[]{:S(2)}) copy-start(f32[8,16,128]{2,1,0:T(8,128)S(1)} %get-tuple-element.18) | copy-start | bytes 196612
  67.3 114.7 %copy-start.6 = (f32[8,16,128]{2,1,0:T(8,128)}, f32[8,16,128]{2,1,0:T(8,128)S(1)}, u32[]{:S(2)}) copy-start(f32[8,16,128]{2,1,0:T(8,128)S(1)} %get-tuple-element.19) | copy-start | bytes 196612
  67.3 114.7 %copy-start.7 = (f32[8,16,128]{2,1,0:T(8,128)}, f32[8,16,128]{2,1,0:T(8,128)S(1)}, u32[]{:S(2)}) copy-start(f32[8,16,128]{2,1,0:T(8,128)S(1)} %get-tuple-element.20) | copy-start | bytes 196612
  67.4 4.8 %collective-permute-start.13 = (f32[1,16,128]{2,1,0:T(8,128)S(1)}, f32[1,16,128]{2,1,0:T(8,128)S(1)}, u32[]{:S(2)}, u32[]{:S(2)}) collective-permute-start(f32[1,16,128]{2,1,0:T(8,128)S(1)} %get-tuple-element.101), channel_id=1, source_target_pairs={{0,4},{4,8},{8,12},{1,5},{5,9},{9,13},{2,6},{6,10},{10,14},{3,7},{... | collective-permute-start | bytes 24584 | tf_op jit(solution)/shard_map/ppermute | solution.py:36
  70.9 5.5 %collective-permute-start.12 = (f32[1,16,128]{2,1,0:T(8,128)S(1)}, f32[1,16,128]{2,1,0:T(8,128)S(1)}, u32[]{:S(2)}, u32[]{:S(2)}) collective-permute-start(f32[1,16,128]{2,1,0:T(8,128)S(1)} %get-tuple-element.102), channel_id=1, source_target_pairs={{4,0},{8,4},{12,8},{5,1},{9,5},{13,9},{6,2},{10,6},{14,10},{7,3},{... | collective-permute-start | bytes 24584 | tf_op jit(solution)/shard_map/ppermute | solution.py:37
  76.5 2.6 %collective-permute-start.15 = (f32[10,1,128]{2,1,0:T(1,128)S(1)}, f32[10,1,128]{2,1,0:T(1,128)S(1)}, u32[]{:S(2)}, u32[]{:S(2)}) collective-permute-start(f32[10,1,128]{2,1,0:T(1,128)S(1)} %get-tuple-element.89), channel_id=1, source_target_pairs={{0,2},{1,3},{4,6},{5,7},{8,10},{9,11},{12,14},{13,15},{16,18},{17,... | collective-permute-start | bytes 15368 | tf_op jit(solution)/shard_map/ppermute | solution.py:36
  77.8 3.1 %collective-permute-start.14 = (f32[10,1,128]{2,1,0:T(1,128)S(1)}, f32[10,1,128]{2,1,0:T(1,128)S(1)}, u32[]{:S(2)}, u32[]{:S(2)}) collective-permute-start(f32[10,1,128]{2,1,0:T(1,128)S(1)} %get-tuple-element.90), channel_id=1, source_target_pairs={{2,0},{3,1},{6,4},{7,5},{10,8},{11,9},{14,12},{15,13},{18,16},{19,... | collective-permute-start | bytes 15368 | tf_op jit(solution)/shard_map/ppermute | solution.py:37
  81.0 7.2 %collective-permute-start.17 = (f32[10,18,1]{2,1,0:T(8,128)S(1)}, f32[10,18,1]{2,1,0:T(8,128)S(1)}, u32[]{:S(2)}, u32[]{:S(2)}) collective-permute-start(f32[10,18,1]{2,1,0:T(8,128)S(1)} %get-tuple-element.55), channel_id=1, source_target_pairs={{0,1},{2,3},{4,5},{6,7},{8,9},{10,11},{12,13},{14,15},{16,17},{18,... | collective-permute-start | bytes 2168 | tf_op jit(solution)/shard_map/ppermute | solution.py:36
  85.3 7.0 %collective-permute-start.16 = (f32[10,18,1]{2,1,0:T(8,128)S(1)}, f32[10,18,1]{2,1,0:T(8,128)S(1)}, u32[]{:S(2)}, u32[]{:S(2)}) collective-permute-start(f32[10,18,1]{2,1,0:T(8,128)S(1)} %get-tuple-element.56), channel_id=1, source_target_pairs={{1,0},{3,2},{5,4},{7,6},{9,8},{11,10},{13,12},{15,14},{17,16},{19,... | collective-permute-start | bytes 2168 | tf_op jit(solution)/shard_map/ppermute | solution.py:37
  92.8 5.0 %collective-permute-start.19 = (f32[1,16,128]{2,1,0:T(8,128)S(1)}, f32[1,16,128]{2,1,0:T(8,128)S(1)}, u32[]{:S(2)}, u32[]{:S(2)}) collective-permute-start(f32[1,16,128]{2,1,0:T(8,128)S(1)} %get-tuple-element.99), channel_id=1, source_target_pairs={{0,4},{4,8},{8,12},{1,5},{5,9},{9,13},{2,6},{6,10},{10,14},{3,7},{... | collective-permute-start | bytes 24584 | tf_op jit(solution)/shard_map/ppermute | solution.py:36
  96.5 5.5 %collective-permute-start.18 = (f32[1,16,128]{2,1,0:T(8,128)S(1)}, f32[1,16,128]{2,1,0:T(8,128)S(1)}, u32[]{:S(2)}, u32[]{:S(2)}) collective-permute-start(f32[1,16,128]{2,1,0:T(8,128)S(1)} %get-tuple-element.100), channel_id=1, source_target_pairs={{4,0},{8,4},{12,8},{5,1},{9,5},{13,9},{6,2},{10,6},{14,10},{7,3},{... | collective-permute-start | bytes 24584 | tf_op jit(solution)/shard_map/ppermute | solution.py:37
  102.0 2.6 %collective-permute-start.21 = (f32[10,1,128]{2,1,0:T(1,128)S(1)}, f32[10,1,128]{2,1,0:T(1,128)S(1)}, u32[]{:S(2)}, u32[]{:S(2)}) collective-permute-start(f32[10,1,128]{2,1,0:T(1,128)S(1)} %get-tuple-element.85), channel_id=1, source_target_pairs={{0,2},{1,3},{4,6},{5,7},{8,10},{9,11},{12,14},{13,15},{16,18},{17,... | collective-permute-start | bytes 15368 | tf_op jit(solution)/shard_map/ppermute | solution.py:36
  103.3 3.1 %collective-permute-start.20 = (f32[10,1,128]{2,1,0:T(1,128)S(1)}, f32[10,1,128]{2,1,0:T(1,128)S(1)}, u32[]{:S(2)}, u32[]{:S(2)}) collective-permute-start(f32[10,1,128]{2,1,0:T(1,128)S(1)} %get-tuple-element.86), channel_id=1, source_target_pairs={{2,0},{3,1},{6,4},{7,5},{10,8},{11,9},{14,12},{15,13},{18,16},{19,... | collective-permute-start | bytes 15368 | tf_op jit(solution)/shard_map/ppermute | solution.py:37
  106.5 4.5 %collective-permute-start.23 = (f32[10,18,1]{2,1,0:T(8,128)S(1)}, f32[10,18,1]{2,1,0:T(8,128)S(1)}, u32[]{:S(2)}, u32[]{:S(2)}) collective-permute-start(f32[10,18,1]{2,1,0:T(8,128)S(1)} %get-tuple-element.53), channel_id=1, source_target_pairs={{0,1},{2,3},{4,5},{6,7},{8,9},{10,11},{12,13},{14,15},{16,17},{18,... | collective-permute-start | bytes 2168 | tf_op jit(solution)/shard_map/ppermute | solution.py:36
  108.0 7.1 %collective-permute-start.22 = (f32[10,18,1]{2,1,0:T(8,128)S(1)}, f32[10,18,1]{2,1,0:T(8,128)S(1)}, u32[]{:S(2)}, u32[]{:S(2)}) collective-permute-start(f32[10,18,1]{2,1,0:T(8,128)S(1)} %get-tuple-element.54), channel_id=1, source_target_pairs={{1,0},{3,2},{5,4},{7,6},{9,8},{11,10},{13,12},{15,14},{17,16},{19,... | collective-permute-start | bytes 2168 | tf_op jit(solution)/shard_map/ppermute | solution.py:37
  115.9 3.3 %collective-permute-start.25 = (f32[1,16,128]{2,1,0:T(8,128)S(1)}, f32[1,16,128]{2,1,0:T(8,128)S(1)}, u32[]{:S(2)}, u32[]{:S(2)}) collective-permute-start(f32[1,16,128]{2,1,0:T(8,128)S(1)} %get-tuple-element.97), channel_id=1, source_target_pairs={{0,4},{4,8},{8,12},{1,5},{5,9},{9,13},{2,6},{6,10},{10,14},{3,7},{... | collective-permute-start | bytes 24584 | tf_op jit(solution)/shard_map/ppermute | solution.py:36
  117.8 5.5 %collective-permute-start.24 = (f32[1,16,128]{2,1,0:T(8,128)S(1)}, f32[1,16,128]{2,1,0:T(8,128)S(1)}, u32[]{:S(2)}, u32[]{:S(2)}) collective-permute-start(f32[1,16,128]{2,1,0:T(8,128)S(1)} %get-tuple-element.98), channel_id=1, source_target_pairs={{4,0},{8,4},{12,8},{5,1},{9,5},{13,9},{6,2},{10,6},{14,10},{7,3},{... | collective-permute-start | bytes 24584 | tf_op jit(solution)/shard_map/ppermute | solution.py:37
  123.4 2.9 %collective-permute-start.27 = (f32[10,1,128]{2,1,0:T(1,128)S(1)}, f32[10,1,128]{2,1,0:T(1,128)S(1)}, u32[]{:S(2)}, u32[]{:S(2)}) collective-permute-start(f32[10,1,128]{2,1,0:T(1,128)S(1)} %get-tuple-element.81), channel_id=1, source_target_pairs={{0,2},{1,3},{4,6},{5,7},{8,10},{9,11},{12,14},{13,15},{16,18},{17,... | collective-permute-start | bytes 15368 | tf_op jit(solution)/shard_map/ppermute | solution.py:36
  124.7 3.2 %collective-permute-start.26 = (f32[10,1,128]{2,1,0:T(1,128)S(1)}, f32[10,1,128]{2,1,0:T(1,128)S(1)}, u32[]{:S(2)}, u32[]{:S(2)}) collective-permute-start(f32[10,1,128]{2,1,0:T(1,128)S(1)} %get-tuple-element.82), channel_id=1, source_target_pairs={{2,0},{3,1},{6,4},{7,5},{10,8},{11,9},{14,12},{15,13},{18,16},{19,... | collective-permute-start | bytes 15368 | tf_op jit(solution)/shard_map/ppermute | solution.py:37
  128.0 4.5 %collective-permute-start.29 = (f32[10,18,1]{2,1,0:T(8,128)S(1)}, f32[10,18,1]{2,1,0:T(8,128)S(1)}, u32[]{:S(2)}, u32[]{:S(2)}) collective-permute-start(f32[10,18,1]{2,1,0:T(8,128)S(1)} %get-tuple-element.51), channel_id=1, source_target_pairs={{0,1},{2,3},{4,5},{6,7},{8,9},{10,11},{12,13},{14,15},{16,17},{18,... | collective-permute-start | bytes 2168 | tf_op jit(solution)/shard_map/ppermute | solution.py:36
  129.4 7.1 %collective-permute-start.28 = (f32[10,18,1]{2,1,0:T(8,128)S(1)}, f32[10,18,1]{2,1,0:T(8,128)S(1)}, u32[]{:S(2)}, u32[]{:S(2)}) collective-permute-start(f32[10,18,1]{2,1,0:T(8,128)S(1)} %get-tuple-element.52), channel_id=1, source_target_pairs={{1,0},{3,2},{5,4},{7,6},{9,8},{11,10},{13,12},{15,14},{17,16},{19,... | collective-permute-start | bytes 2168 | tf_op jit(solution)/shard_map/ppermute | solution.py:37
  137.4 4.0 %collective-permute-start.31 = (f32[1,16,128]{2,1,0:T(8,128)S(1)}, f32[1,16,128]{2,1,0:T(8,128)S(1)}, u32[]{:S(2)}, u32[]{:S(2)}) collective-permute-start(f32[1,16,128]{2,1,0:T(8,128)S(1)} %get-tuple-element.95), channel_id=1, source_target_pairs={{0,4},{4,8},{8,12},{1,5},{5,9},{9,13},{2,6},{6,10},{10,14},{3,7},{... | collective-permute-start | bytes 24584 | tf_op jit(solution)/shard_map/ppermute | solution.py:36
  139.3 5.5 %collective-permute-start.30 = (f32[1,16,128]{2,1,0:T(8,128)S(1)}, f32[1,16,128]{2,1,0:T(8,128)S(1)}, u32[]{:S(2)}, u32[]{:S(2)}) collective-permute-start(f32[1,16,128]{2,1,0:T(8,128)S(1)} %get-tuple-element.96), channel_id=1, source_target_pairs={{4,0},{8,4},{12,8},{5,1},{9,5},{13,9},{6,2},{10,6},{14,10},{7,3},{... | collective-permute-start | bytes 24584 | tf_op jit(solution)/shard_map/ppermute | solution.py:37
  144.9 3.6 %collective-permute-start.33 = (f32[10,1,128]{2,1,0:T(1,128)S(1)}, f32[10,1,128]{2,1,0:T(1,128)S(1)}, u32[]{:S(2)}, u32[]{:S(2)}) collective-permute-start(f32[10,1,128]{2,1,0:T(1,128)S(1)} %get-tuple-element.77), channel_id=1, source_target_pairs={{0,2},{1,3},{4,6},{5,7},{8,10},{9,11},{12,14},{13,15},{16,18},{17,... | collective-permute-start | bytes 15368 | tf_op jit(solution)/shard_map/ppermute | solution.py:36
  146.2 3.1 %collective-permute-start.32 = (f32[10,1,128]{2,1,0:T(1,128)S(1)}, f32[10,1,128]{2,1,0:T(1,128)S(1)}, u32[]{:S(2)}, u32[]{:S(2)}) collective-permute-start(f32[10,1,128]{2,1,0:T(1,128)S(1)} %get-tuple-element.78), channel_id=1, source_target_pairs={{2,0},{3,1},{6,4},{7,5},{10,8},{11,9},{14,12},{15,13},{18,16},{19,... | collective-permute-start | bytes 15368 | tf_op jit(solution)/shard_map/ppermute | solution.py:37
  149.4 4.7 %collective-permute-start.35 = (f32[10,18,1]{2,1,0:T(8,128)S(1)}, f32[10,18,1]{2,1,0:T(8,128)S(1)}, u32[]{:S(2)}, u32[]{:S(2)}) collective-permute-start(f32[10,18,1]{2,1,0:T(8,128)S(1)} %get-tuple-element.49), channel_id=1, source_target_pairs={{0,1},{2,3},{4,5},{6,7},{8,9},{10,11},{12,13},{14,15},{16,17},{18,... | collective-permute-start | bytes 2168 | tf_op jit(solution)/shard_map/ppermute | solution.py:36
  150.8 7.3 %collective-permute-start.34 = (f32[10,18,1]{2,1,0:T(8,128)S(1)}, f32[10,18,1]{2,1,0:T(8,128)S(1)}, u32[]{:S(2)}, u32[]{:S(2)}) collective-permute-start(f32[10,18,1]{2,1,0:T(8,128)S(1)} %get-tuple-element.50), channel_id=1, source_target_pairs={{1,0},{3,2},{5,4},{7,6},{9,8},{11,10},{13,12},{15,14},{17,16},{19,... | collective-permute-start | bytes 2168 | tf_op jit(solution)/shard_map/ppermute | solution.py:37
  159.3 3.8 %collective-permute-start.37 = (f32[1,16,128]{2,1,0:T(8,128)S(1)}, f32[1,16,128]{2,1,0:T(8,128)S(1)}, u32[]{:S(2)}, u32[]{:S(2)}) collective-permute-start(f32[1,16,128]{2,1,0:T(8,128)S(1)} %get-tuple-element.93), channel_id=1, source_target_pairs={{0,4},{4,8},{8,12},{1,5},{5,9},{9,13},{2,6},{6,10},{10,14},{3,7},{... | collective-permute-start | bytes 24584 | tf_op jit(solution)/shard_map/ppermute | solution.py:36
  161.2 5.5 %collective-permute-start.36 = (f32[1,16,128]{2,1,0:T(8,128)S(1)}, f32[1,16,128]{2,1,0:T(8,128)S(1)}, u32[]{:S(2)}, u32[]{:S(2)}) collective-permute-start(f32[1,16,128]{2,1,0:T(8,128)S(1)} %get-tuple-element.94), channel_id=1, source_target_pairs={{4,0},{8,4},{12,8},{5,1},{9,5},{13,9},{6,2},{10,6},{14,10},{7,3},{... | collective-permute-start | bytes 24584 | tf_op jit(solution)/shard_map/ppermute | solution.py:37
  166.7 3.6 %collective-permute-start.39 = (f32[10,1,128]{2,1,0:T(1,128)S(1)}, f32[10,1,128]{2,1,0:T(1,128)S(1)}, u32[]{:S(2)}, u32[]{:S(2)}) collective-permute-start(f32[10,1,128]{2,1,0:T(1,128)S(1)} %get-tuple-element.73), channel_id=1, source_target_pairs={{0,2},{1,3},{4,6},{5,7},{8,10},{9,11},{12,14},{13,15},{16,18},{17,... | collective-permute-start | bytes 15368 | tf_op jit(solution)/shard_map/ppermute | solution.py:36
  168.0 3.1 %collective-permute-start.38 = (f32[10,1,128]{2,1,0:T(1,128)S(1)}, f32[10,1,128]{2,1,0:T(1,128)S(1)}, u32[]{:S(2)}, u32[]{:S(2)}) collective-permute-start(f32[10,1,128]{2,1,0:T(1,128)S(1)} %get-tuple-element.74), channel_id=1, source_target_pairs={{2,0},{3,1},{6,4},{7,5},{10,8},{11,9},{14,12},{15,13},{18,16},{19,... | collective-permute-start | bytes 15368 | tf_op jit(solution)/shard_map/ppermute | solution.py:37
  171.2 4.8 %collective-permute-start.41 = (f32[10,18,1]{2,1,0:T(8,128)S(1)}, f32[10,18,1]{2,1,0:T(8,128)S(1)}, u32[]{:S(2)}, u32[]{:S(2)}) collective-permute-start(f32[10,18,1]{2,1,0:T(8,128)S(1)} %get-tuple-element.47), channel_id=1, source_target_pairs={{0,1},{2,3},{4,5},{6,7},{8,9},{10,11},{12,13},{14,15},{16,17},{18,... | collective-permute-start | bytes 2168 | tf_op jit(solution)/shard_map/ppermute | solution.py:36
  172.7 7.4 %collective-permute-start.40 = (f32[10,18,1]{2,1,0:T(8,128)S(1)}, f32[10,18,1]{2,1,0:T(8,128)S(1)}, u32[]{:S(2)}, u32[]{:S(2)}) collective-permute-start(f32[10,18,1]{2,1,0:T(8,128)S(1)} %get-tuple-element.48), channel_id=1, source_target_pairs={{1,0},{3,2},{5,4},{7,6},{9,8},{11,10},{13,12},{15,14},{17,16},{19,... | collective-permute-start | bytes 2168 | tf_op jit(solution)/shard_map/ppermute | solution.py:37
  (50 other events, 2073.9 us)
where the time goes:
time: 219 us; the launch traced here: 217 us
  starting transfers between devices  78.7 us (36%)
  waiting for transfers between devices  62.6 us (29%)
  blocking collectives  29.5 us (13%)
  other arithmetic  28.1 us (13%)
  local copies, waits for them, and re-layouts  13.7 us (6%)
  matrix products  2.53 us (1%)
  between operations  2.23 us (1%)
    ppermute x21, waiting for transfers between devices, extended(): after = lax.ppermute(initial, axis, down)  51.3 us
    ppermute x21, starting transfers between devices, extended(): before = lax.ppermute(last, axis, up)  51.3 us
    psum x1, blocking collectives, local(): total = total + lax.psum(partial_sums, ('gx', 'gy', 'gz'))  29.5 us
    ppermute x21, starting transfers between devices, extended(): after = lax.ppermute(initial, axis, down)  27.4 us
    mul x2, other arithmetic, local_coefficients(): flux_local = (tissue_local * local_factor)[None] * fibre_local  12.1 us
    ppermute x21, waiting for transfers between devices, extended(): before = lax.ppermute(last, axis, up)  11.3 us
  transfers between devices with their start and end apart: 42, of which 23 were waited for; matrix products, arithmetic and copies ran while one was open for 12% of the time, Pallas kernels for 0%

commit v1 on v0

--- a/solution.py
+++ b/solution.py
@@ -171,7 +171,7 @@
         partial_sums = jnp.einsum(
             "rxyz,xyz->r", selector, terms, precision=jax.lax.Precision.HIGHEST
         )
-        total = total + lax.psum(partial_sums, ("gx", "gy", "gz"))
+        total = total + jnp.sum(lax.all_gather(partial_sums, ("gx", "gy", "gz")), axis=0)
         deriv_vv, deriv_vh, deriv_hv, deriv_hh = ionic_partials(
             crop(volts_pad, 1), saved_gates[step]
         )

time: 219 us -> 230 us (1.050)
  waiting for transfers between devices: 62.6 us -> 26.8 us
  starting transfers between devices: 78.7 us -> 109 us
  other arithmetic: 28.1 us -> 37.1 us
  blocking collectives: 29.5 us -> 32.9 us
    ppermute x21, waiting for transfers between devices: 51.3 us -> 13.8 us  [extended(): after = lax.ppermute(initial, axis, down)]
    unnamed x0 -> x1, blocking collectives: none -> 32.9 us
    ppermute x21, starting transfers between devices: 51.3 us -> 81.2 us  [extended(): before = lax.ppermute(last, axis, up)]
    psum x1 -> x0, blocking collectives: 29.5 us -> none  [local(): total = total + lax.psum(partial_sums, ('gx', 'gy', 'gz'))]
    mul x3, other arithmetic: 2.05 us -> 5.63 us  [local(): masked = tissue_local * back_v]
    concatenate x24, other arithmetic: 4.09 us -> 7.27 us  [extended(): array = jnp.concatenate([before, array, after], axis=dim)]
    unnamed x116 -> x273, local copies, waits for them, and re-layouts: 4 us -> 6.55 us
  transfers between devices with their start and end apart: 42 -> 42, of which waited for: 23 -> 19; matrix products, arithmetic and copies ran while one was open for 12% -> 13% of each run, Pallas kernels for 0% -> 0%
where the time goes in v1:
time: 230 us; the launch traced here: 228 us
  starting transfers between devices  109 us (47%)
  other arithmetic  37.1 us (16%)
  blocking collectives  32.9 us (14%)
  waiting for transfers between devices  26.8 us (12%)
  local copies, waits for them, and re-layouts  14.9 us (6%)
  between operations  4.08 us (2%)
  matrix products  3.34 us (1%)
    ppermute x21, starting transfers between devices, extended(): before = lax.ppermute(last, axis, up)  81.2 us
    unnamed x1, blocking collectives  32.9 us
    ppermute x21, starting transfers between devices, extended(): after = lax.ppermute(initial, axis, down)  27.7 us
    ppermute x21, waiting for transfers between devices, extended(): after = lax.ppermute(initial, axis, down)  13.8 us
    ppermute x21, waiting for transfers between devices, extended(): before = lax.ppermute(last, axis, up)  13.1 us
    mul x2, other arithmetic, local_coefficients(): flux_local = (tissue_local * local_factor)[None] * fibre_local  12.1 us
    concatenate x24, other arithmetic, extended(): array = jnp.concatenate([before, array, after], axis=dim)  7.27 us
    unnamed x273, local copies, waits for them, and re-layouts  6.55 us
  transfers between devices with their start and end apart: 42, of which 19 were waited for; matrix products, arithmetic and copies ran while one was open for 13% of the time, Pallas kernels for 0%

profile of v1, /device:TPU:0, one launch (start us, length us, event | category | flops | bytes accessed | tf_op | source)
XLA Modules:
  0.0 228.1 jit_solution(17368695246881135488)
XLA Ops:
  1.4 4.9 %collective-permute-start.7 = (f32[1,16,128]{2,1,0:T(8,128)S(1)}, f32[1,16,128]{2,1,0:T(8,128)S(1)}, u32[]{:S(2)}, u32[]{:S(2)}) collective-permute-start(f32[1,16,128]{2,1,0:T(8,128)S(1)} %get-tuple-element.118), channel_id=1, source_target_pairs={{0,4},{4,8},{8,12},{1,5},{5,9},{9,13},{2,6},{6,10},{10,14},{3,7},{... | collective-permute-start | bytes 24584 | tf_op jit(solution)/shard_map/ppermute | solution.py:36
  6.4 1.3 collective-permute-start.6
  7.7 2.0 fusion.196
  11.6 11.0 %add_multiply_fusion.3 = f32[8,16,128]{2,1,0:T(8,128)S(1)} fusion(s32[8,16,128]{2,1,0:T(8,128)} %param.15, s32[8,16,128]{2,1,0:T(8,128)} %param.17, f32[]{:T(128)} %bitcast.15, f32[]{:T(128)} %bitcast.14, f32[]{:T(128)} %bitcast.13, f32[]{:T(128)} %bitcast.12, f32[]{:T(128)} %bitcast.11, f32[]{:T(128)} %bitcast.10, f32[]{:T(128)} %bitcast.9, f32[]{:T(128)} %bitcast.8, ...), kind=kLoop, calls=%fused_computation.358 | loop fusion | flops 802816 | bytes 196672 | tf_op jit(solution)/shard_map/mul | solution.py:126
  23.8 1.3 collective-permute-start.8
  25.1 3.0 %collective-permute-start.9 = (f32[10,1,128]{2,1,0:T(1,128)S(1)}, f32[10,1,128]{2,1,0:T(1,128)S(1)}, u32[]{:S(2)}, u32[]{:S(2)}) collective-permute-start(f32[10,1,128]{2,1,0:T(1,128)S(1)} %get-tuple-element.94), channel_id=1, source_target_pairs={{0,2},{1,3},{4,6},{5,7},{8,10},{9,11},{12,14},{13,15},{16,18},{17,... | collective-permute-start | bytes 15368 | tf_op jit(solution)/shard_map/ppermute | solution.py:36
  28.1 4.5 %collective-permute-start = (f32[9,1,16,128]{3,2,1,0:T(8,128)S(1)}, f32[9,1,16,128]{3,2,1,0:T(8,128)S(1)}, u32[]{:S(2)}, u32[]{:S(2)}) collective-permute-start(f32[9,1,16,128]{3,2,1,0:T(8,128)S(1)} %get-tuple-element.48), channel_id=1, source_target_pairs={{0,4},{4,8},{8,12},{1,5},{5,9},{9,13},{2,6},{6,10},{10,14},{3,7},{... | collective-permute-start | bytes 221192 | tf_op jit(solution)/shard_map/ppermute | solution.py:36
  34.7 4.3 %collective-permute-done.1 = f32[9,1,16,128]{3,2,1,0:T(8,128)S(1)} collective-permute-done((f32[9,1,16,128]{3,2,1,0:T(8,128)S(1)}, f32[9,1,16,128]{3,2,1,0:T(8,128)S(1)}, u32[]{:S(2)}, u32[]{:S(2)}) %collective-permute-start.1) | collective-permute-done | bytes 73760 | tf_op jit(solution)/shard_map/ppermute | solution.py:37
  39.0 1.3 collective-permute-start.2
  43.0 4.6 %collective-permute-start.11 = (f32[10,18,1]{2,1,0:T(8,128)S(1)}, f32[10,18,1]{2,1,0:T(8,128)S(1)}, u32[]{:S(2)}, u32[]{:S(2)}) collective-permute-start(f32[10,18,1]{2,1,0:T(8,128)S(1)} %get-tuple-element.60), channel_id=1, source_target_pairs={{0,1},{2,3},{4,5},{6,7},{8,9},{10,11},{12,13},{14,15},{16,17},{18,... | collective-permute-start | bytes 2168 | tf_op jit(solution)/shard_map/ppermute | solution.py:36
  47.8 1.4 fusion.181
  49.1 1.9 copy.170
  55.8 3.1 %collective-permute-done.5 = f32[9,10,18,1]{2,3,1,0:T(1,128)S(1)} collective-permute-done((f32[9,10,18,1]{2,3,1,0:T(1,128)S(1)}, f32[9,10,18,1]{2,3,1,0:T(1,128)S(1)}, u32[]{:S(2)}, u32[]{:S(2)}) %collective-permute-start.5) | collective-permute-done | bytes 6512 | tf_op jit(solution)/shard_map/ppermute | solution.py:37
  59.0 1.7 copy.162
  60.6 2.6 %pad_maximum_fusion = f32[9,10,18,130]{3,2,1,0:T(8,128)S(1)} fusion(f32[9,10,18,1]{3,2,1,0:T(8,128)} %copy.162, f32[9,10,1,128]{3,2,1,0:T(1,128)S(1)} %collective-permute-done.3, f32[9,1,16,128]{3,2,1,0:T(8,128)S(1)} %collective-permute-done.1, f32[9,8,16,128]{3,2,1,0:T(8,128)S(1)} %get-tuple-element.33, f32[9,1,16,128]{3,2,1,0:T(8,128)S(1)} %collective-permute-done, ...), kind=kLoop, calls=%fused_computation | loop fusion | flops 1263600 | bytes 1684800 | tf_op jit(solution)/shard_map/concatenate | solution.py:38
  66.7 4.5 %collective-permute-start.13 = (f32[1,16,128]{2,1,0:T(8,128)S(1)}, f32[1,16,128]{2,1,0:T(8,128)S(1)}, u32[]{:S(2)}, u32[]{:S(2)}) collective-permute-start(f32[1,16,128]{2,1,0:T(8,128)S(1)} %get-tuple-element.104), channel_id=1, source_target_pairs={{0,4},{4,8},{8,12},{1,5},{5,9},{9,13},{2,6},{6,10},{10,14},{3,7},{... | collective-permute-start | bytes 24584 | tf_op jit(solution)/shard_map/ppermute | solution.py:36
  71.2 1.3 collective-permute-done.13
  73.9 3.0 %collective-permute-start.15 = (f32[10,1,128]{2,1,0:T(1,128)S(1)}, f32[10,1,128]{2,1,0:T(1,128)S(1)}, u32[]{:S(2)}, u32[]{:S(2)}) collective-permute-start(f32[10,1,128]{2,1,0:T(1,128)S(1)} %get-tuple-element.92), channel_id=1, source_target_pairs={{0,2},{1,3},{4,6},{5,7},{8,10},{9,11},{12,14},{13,15},{16,18},{17,... | collective-permute-start | bytes 15368 | tf_op jit(solution)/shard_map/ppermute | solution.py:36
  79.2 4.6 %collective-permute-start.17 = (f32[10,18,1]{2,1,0:T(8,128)S(1)}, f32[10,18,1]{2,1,0:T(8,128)S(1)}, u32[]{:S(2)}, u32[]{:S(2)}) collective-permute-start(f32[10,18,1]{2,1,0:T(8,128)S(1)} %get-tuple-element.58), channel_id=1, source_target_pairs={{0,1},{2,3},{4,5},{6,7},{8,9},{10,11},{12,13},{14,15},{16,17},{18,... | collective-permute-start | bytes 2168 | tf_op jit(solution)/shard_map/ppermute | solution.py:36
  83.8 1.6 collective-permute-done.16
  87.0 1.4 collective-permute-start.18
  88.4 4.8 %collective-permute-start.19 = (f32[1,16,128]{2,1,0:T(8,128)S(1)}, f32[1,16,128]{2,1,0:T(8,128)S(1)}, u32[]{:S(2)}, u32[]{:S(2)}) collective-permute-start(f32[1,16,128]{2,1,0:T(8,128)S(1)} %get-tuple-element.102), channel_id=1, source_target_pairs={{0,4},{4,8},{8,12},{1,5},{5,9},{9,13},{2,6},{6,10},{10,14},{3,7},{... | collective-permute-start | bytes 24584 | tf_op jit(solution)/shard_map/ppermute | solution.py:36
  93.3 1.3 collective-permute-done.19
  95.9 3.0 %collective-permute-start.21 = (f32[10,1,128]{2,1,0:T(1,128)S(1)}, f32[10,1,128]{2,1,0:T(1,128)S(1)}, u32[]{:S(2)}, u32[]{:S(2)}) collective-permute-start(f32[10,1,128]{2,1,0:T(1,128)S(1)} %get-tuple-element.88), channel_id=1, source_target_pairs={{0,2},{1,3},{4,6},{5,7},{8,10},{9,11},{12,14},{13,15},{16,18},{17,... | collective-permute-start | bytes 15368 | tf_op jit(solution)/shard_map/ppermute | solution.py:36
  101.2 4.6 %collective-permute-start.23 = (f32[10,18,1]{2,1,0:T(8,128)S(1)}, f32[10,18,1]{2,1,0:T(8,128)S(1)}, u32[]{:S(2)}, u32[]{:S(2)}) collective-permute-start(f32[10,18,1]{2,1,0:T(8,128)S(1)} %get-tuple-element.56), channel_id=1, source_target_pairs={{0,1},{2,3},{4,5},{6,7},{8,9},{10,11},{12,13},{14,15},{16,17},{18,... | collective-permute-start | bytes 2168 | tf_op jit(solution)/shard_map/ppermute | solution.py:36
  105.8 1.7 collective-permute-done.22
  111.5 4.8 %collective-permute-start.25 = (f32[1,16,128]{2,1,0:T(8,128)S(1)}, f32[1,16,128]{2,1,0:T(8,128)S(1)}, u32[]{:S(2)}, u32[]{:S(2)}) collective-permute-start(f32[1,16,128]{2,1,0:T(8,128)S(1)} %get-tuple-element.100), channel_id=1, source_target_pairs={{0,4},{4,8},{8,12},{1,5},{5,9},{9,13},{2,6},{6,10},{10,14},{3,7},{... | collective-permute-start | bytes 24584 | tf_op jit(solution)/shard_map/ppermute | solution.py:36
  116.3 1.3 collective-permute-done.25
  119.0 3.0 %collective-permute-start.27 = (f32[10,1,128]{2,1,0:T(1,128)S(1)}, f32[10,1,128]{2,1,0:T(1,128)S(1)}, u32[]{:S(2)}, u32[]{:S(2)}) collective-permute-start(f32[10,1,128]{2,1,0:T(1,128)S(1)} %get-tuple-element.84), channel_id=1, source_target_pairs={{0,2},{1,3},{4,6},{5,7},{8,10},{9,11},{12,14},{13,15},{16,18},{17,... | collective-permute-start | bytes 15368 | tf_op jit(solution)/shard_map/ppermute | solution.py:36
  125.6 4.6 %collective-permute-start.29 = (f32[10,18,1]{2,1,0:T(8,128)S(1)}, f32[10,18,1]{2,1,0:T(8,128)S(1)}, u32[]{:S(2)}, u32[]{:S(2)}) collective-permute-start(f32[10,18,1]{2,1,0:T(8,128)S(1)} %get-tuple-element.54), channel_id=1, source_target_pairs={{0,1},{2,3},{4,5},{6,7},{8,9},{10,11},{12,13},{14,15},{16,17},{18,... | collective-permute-start | bytes 2168 | tf_op jit(solution)/shard_map/ppermute | solution.py:36
  131.0 1.5 collective-permute-done.29
  132.9 1.9 convert_multiply_fusion
  136.2 4.8 %collective-permute-start.31 = (f32[1,16,128]{2,1,0:T(8,128)S(1)}, f32[1,16,128]{2,1,0:T(8,128)S(1)}, u32[]{:S(2)}, u32[]{:S(2)}) collective-permute-start(f32[1,16,128]{2,1,0:T(8,128)S(1)} %get-tuple-element.98), channel_id=1, source_target_pairs={{0,4},{4,8},{8,12},{1,5},{5,9},{9,13},{2,6},{6,10},{10,14},{3,7},{... | collective-permute-start | bytes 24584 | tf_op jit(solution)/shard_map/ppermute | solution.py:36
  143.2 1.6 collective-permute-start.32
  144.8 3.0 %collective-permute-start.33 = (f32[10,1,128]{2,1,0:T(1,128)S(1)}, f32[10,1,128]{2,1,0:T(1,128)S(1)}, u32[]{:S(2)}, u32[]{:S(2)}) collective-permute-start(f32[10,1,128]{2,1,0:T(1,128)S(1)} %get-tuple-element.80), channel_id=1, source_target_pairs={{0,2},{1,3},{4,6},{5,7},{8,10},{9,11},{12,14},{13,15},{16,18},{17,... | collective-permute-start | bytes 15368 | tf_op jit(solution)/shard_map/ppermute | solution.py:36
  151.0 4.6 %collective-permute-start.35 = (f32[10,18,1]{2,1,0:T(8,128)S(1)}, f32[10,18,1]{2,1,0:T(8,128)S(1)}, u32[]{:S(2)}, u32[]{:S(2)}) collective-permute-start(f32[10,18,1]{2,1,0:T(8,128)S(1)} %get-tuple-element.52), channel_id=1, source_target_pairs={{0,1},{2,3},{4,5},{6,7},{8,9},{10,11},{12,13},{14,15},{16,17},{18,... | collective-permute-start | bytes 2168 | tf_op jit(solution)/shard_map/ppermute | solution.py:36
  155.6 1.4 collective-permute-done.34
  159.5 2.5 %convert_multiply_fusion.2 = f32[8,16,128]{2,1,0:T(8,128)S(1)} fusion(s32[8,16,128]{2,1,0:T(8,128)} %param.15, f32[8,16,128]{2,1,0:T(8,128)} %param.13, f32[8,16,128]{2,1,0:T(8,128)S(1)} %get-tuple-element.12, f32[8,16,128]{2,1,0:T(8,128)} %param.12, f32[8,16,128]{2,1,0:T(8,128)} %param.14, f32[8,16,128]{2,1,0:T(8,128)} %copy-done.65, ...), kind=kLoop, calls=%fused_computation.361 | loop fusion | flops 4161536 | bytes 5029888 | tf_op jit(solution)/shard_map/mul | solution.py:167
  163.4 4.7 %collective-permute-start.37 = (f32[1,16,128]{2,1,0:T(8,128)S(1)}, f32[1,16,128]{2,1,0:T(8,128)S(1)}, u32[]{:S(2)}, u32[]{:S(2)}) collective-permute-start(f32[1,16,128]{2,1,0:T(8,128)S(1)} %get-tuple-element.96), channel_id=1, source_target_pairs={{0,4},{4,8},{8,12},{1,5},{5,9},{9,13},{2,6},{6,10},{10,14},{3,7},{... | collective-permute-start | bytes 24584 | tf_op jit(solution)/shard_map/ppermute | solution.py:36
  168.4 1.7 fusion.18
  171.4 1.4 collective-permute-start.38
  172.8 3.0 %collective-permute-start.39 = (f32[10,1,128]{2,1,0:T(1,128)S(1)}, f32[10,1,128]{2,1,0:T(1,128)S(1)}, u32[]{:S(2)}, u32[]{:S(2)}) collective-permute-start(f32[10,1,128]{2,1,0:T(1,128)S(1)} %get-tuple-element.76), channel_id=1, source_target_pairs={{0,2},{1,3},{4,6},{5,7},{8,10},{9,11},{12,14},{13,15},{16,18},{17,... | collective-permute-start | bytes 15368 | tf_op jit(solution)/shard_map/ppermute | solution.py:36
  175.9 1.7 convolution_bitcast_fusion.1
  180.2 4.6 %collective-permute-start.41 = (f32[10,18,1]{2,1,0:T(8,128)S(1)}, f32[10,18,1]{2,1,0:T(8,128)S(1)}, u32[]{:S(2)}, u32[]{:S(2)}) collective-permute-start(f32[10,18,1]{2,1,0:T(8,128)S(1)} %get-tuple-element.50), channel_id=1, source_target_pairs={{0,1},{2,3},{4,5},{6,7},{8,9},{10,11},{12,13},{14,15},{16,17},{18,... | collective-permute-start | bytes 2168 | tf_op jit(solution)/shard_map/ppermute | solution.py:36
  185.6 1.5 collective-permute-done.41
  187.5 2.1 add_multiply_fusion
  190.6 32.9 %all-reduce.3 = (f32[256]{0:T(256)S(1)}, f32[256]{0:T(256)S(1)}, f32[256]{0:T(256)S(1)}) all-reduce(f32[256]{0:T(256)S(1)} %dynamic-update-slice.2, f32[256]{0:T(256)} %copy-done.128, f32[256]{0:T(256)} %copy-done.129), channel_id=4, replica_groups=mesh['twin'=2,'gx'=4,'gy'=2,'gz'=2] {'gx','gy','gz'}, use_global_device_ids=true, to_apply=%add.2 | all-reduce | flops 768 | bytes 6144
  224.4 3.5 %fusion.12 = f32[8,16,128]{2,1,0:T(8,128)} fusion(f32[8,16,128]{2,1,0:T(8,128)} %param.11, f32[8,16,128]{2,1,0:T(8,128)} %param.10, f32[8,16,128]{2,1,0:T(8,128)} %copy-done.48, f32[8,16,128]{2,1,0:T(8,128)} %copy-done.45, f32[8,16,128]{2,1,0:T(8,128)} %copy-done.42, f32[8,16,128]{2,1,0:T(8,128)} %copy-done.39, f32[8,16,128]{2,1,0:T(8,128)} %copy-done.36, ...), kind=kLoop, calls=%fused_computation.80 | loop fusion | flops 5701632 | bytes 6291456 | tf_op jit(solution)/shard_map/add | solution.py:180
  (381 shorter events, 51.2 us)
Async XLA Ops:
  1.4 22.3 %collective-permute-start.7 = (f32[1,16,128]{2,1,0:T(8,128)S(1)}, f32[1,16,128]{2,1,0:T(8,128)S(1)}, u32[]{:S(2)}, u32[]{:S(2)}) collective-permute-start(f32[1,16,128]{2,1,0:T(8,128)S(1)} %get-tuple-element.118), channel_id=1, source_target_pairs={{0,4},{4,8},{8,12},{1,5},{5,9},{9,13},{2,6},{6,10},{10,14},{3,7},{... | collective-permute-start | bytes 24584 | tf_op jit(solution)/shard_map/ppermute | solution.py:36
  6.4 17.4 %collective-permute-start.6 = (f32[1,16,128]{2,1,0:T(8,128)S(1)}, f32[1,16,128]{2,1,0:T(8,128)S(1)}, u32[]{:S(2)}, u32[]{:S(2)}) collective-permute-start(f32[1,16,128]{2,1,0:T(8,128)S(1)} %get-tuple-element.119), channel_id=1, source_target_pairs={{4,0},{8,4},{12,8},{5,1},{9,5},{13,9},{6,2},{10,6},{14,10},{7,3},{... | collective-permute-start | bytes 24584 | tf_op jit(solution)/shard_map/ppermute | solution.py:37
  23.8 10.2 %collective-permute-start.8 = (f32[10,1,128]{2,1,0:T(1,128)S(1)}, f32[10,1,128]{2,1,0:T(1,128)S(1)}, u32[]{:S(2)}, u32[]{:S(2)}) collective-permute-start(f32[10,1,128]{2,1,0:T(1,128)S(1)} %get-tuple-element.95), channel_id=1, source_target_pairs={{2,0},{3,1},{6,4},{7,5},{10,8},{11,9},{14,12},{15,13},{18,16},{19,... | collective-permute-start | bytes 15368 | tf_op jit(solution)/shard_map/ppermute | solution.py:37
  25.1 9.0 %collective-permute-start.9 = (f32[10,1,128]{2,1,0:T(1,128)S(1)}, f32[10,1,128]{2,1,0:T(1,128)S(1)}, u32[]{:S(2)}, u32[]{:S(2)}) collective-permute-start(f32[10,1,128]{2,1,0:T(1,128)S(1)} %get-tuple-element.94), channel_id=1, source_target_pairs={{0,2},{1,3},{4,6},{5,7},{8,10},{9,11},{12,14},{13,15},{16,18},{17,... | collective-permute-start | bytes 15368 | tf_op jit(solution)/shard_map/ppermute | solution.py:36
  28.1 6.5 %collective-permute-start = (f32[9,1,16,128]{3,2,1,0:T(8,128)S(1)}, f32[9,1,16,128]{3,2,1,0:T(8,128)S(1)}, u32[]{:S(2)}, u32[]{:S(2)}) collective-permute-start(f32[9,1,16,128]{3,2,1,0:T(8,128)S(1)} %get-tuple-element.48), channel_id=1, source_target_pairs={{0,4},{4,8},{8,12},{1,5},{5,9},{9,13},{2,6},{6,10},{10,14},{3,7},{... | collective-permute-start | bytes 221192 | tf_op jit(solution)/shard_map/ppermute | solution.py:36
  32.7 6.2 %collective-permute-start.1 = (f32[9,1,16,128]{3,2,1,0:T(8,128)S(1)}, f32[9,1,16,128]{3,2,1,0:T(8,128)S(1)}, u32[]{:S(2)}, u32[]{:S(2)}) collective-permute-start(f32[9,1,16,128]{3,2,1,0:T(8,128)S(1)} %get-tuple-element.49), channel_id=1, source_target_pairs={{4,0},{8,4},{12,8},{5,1},{9,5},{13,9},{6,2},{10,6},{14,10},{7,3},{... | collective-permute-start | bytes 221192 | tf_op jit(solution)/shard_map/ppermute | solution.py:37
  39.0 8.6 %collective-permute-start.2 = (f32[9,10,1,128]{3,2,1,0:T(1,128)S(1)}, f32[9,10,1,128]{3,2,1,0:T(1,128)S(1)}, u32[]{:S(2)}, u32[]{:S(2)}) collective-permute-start(f32[9,10,1,128]{3,2,1,0:T(1,128)S(1)} %get-tuple-element.46), channel_id=1, source_target_pairs={{0,2},{1,3},{4,6},{5,7},{8,10},{9,11},{12,14},{13,15},{16,18},{17,... | collective-permute-start | bytes 138248 | tf_op jit(solution)/shard_map/ppermute | solution.py:36
  40.3 7.3 %collective-permute-start.3 = (f32[9,10,1,128]{3,2,1,0:T(1,128)S(1)}, f32[9,10,1,128]{3,2,1,0:T(1,128)S(1)}, u32[]{:S(2)}, u32[]{:S(2)}) collective-permute-start(f32[9,10,1,128]{3,2,1,0:T(1,128)S(1)} %get-tuple-element.47), channel_id=1, source_target_pairs={{2,0},{3,1},{6,4},{7,5},{10,8},{11,9},{14,12},{15,13},{18,16},{19,... | collective-permute-start | bytes 138248 | tf_op jit(solution)/shard_map/ppermute | solution.py:37
  41.7 12.5 %collective-permute-start.10 = (f32[10,18,1]{2,1,0:T(8,128)S(1)}, f32[10,18,1]{2,1,0:T(8,128)S(1)}, u32[]{:S(2)}, u32[]{:S(2)}) collective-permute-start(f32[10,18,1]{2,1,0:T(8,128)S(1)} %get-tuple-element.61), channel_id=1, source_target_pairs={{1,0},{3,2},{5,4},{7,6},{9,8},{11,10},{13,12},{15,14},{17,16},{19,... | collective-permute-start | bytes 2168 | tf_op jit(solution)/shard_map/ppermute | solution.py:37
  43.0 11.2 %collective-permute-start.11 = (f32[10,18,1]{2,1,0:T(8,128)S(1)}, f32[10,18,1]{2,1,0:T(8,128)S(1)}, u32[]{:S(2)}, u32[]{:S(2)}) collective-permute-start(f32[10,18,1]{2,1,0:T(8,128)S(1)} %get-tuple-element.60), channel_id=1, source_target_pairs={{0,1},{2,3},{4,5},{6,7},{8,9},{10,11},{12,13},{14,15},{16,17},{18,... | collective-permute-start | bytes 2168 | tf_op jit(solution)/shard_map/ppermute | solution.py:36
  51.0 4.2 %collective-permute-start.4 = (f32[9,10,18,1]{2,3,1,0:T(1,128)S(1)}, f32[9,10,18,1]{2,3,1,0:T(1,128)S(1)}, u32[]{:S(2)}, u32[]{:S(2)}) collective-permute-start(f32[9,10,18,1]{2,3,1,0:T(1,128)S(1)} %copy.170), channel_id=1, source_target_pairs={{0,1},{2,3},{4,5},{6,7},{8,9},{10,11},{12,13},{14,15},{16,17},{18,... | collective-permute-start | bytes 19448 | tf_op jit(solution)/shard_map/ppermute | solution.py:36
  52.9 6.0 %collective-permute-start.5 = (f32[9,10,18,1]{2,3,1,0:T(1,128)S(1)}, f32[9,10,18,1]{2,3,1,0:T(1,128)S(1)}, u32[]{:S(2)}, u32[]{:S(2)}) collective-permute-start(f32[9,10,18,1]{2,3,1,0:T(1,128)S(1)} %copy.171), channel_id=1, source_target_pairs={{1,0},{3,2},{5,4},{7,6},{9,8},{11,10},{13,12},{15,14},{17,16},{19,... | collective-permute-start | bytes 19448 | tf_op jit(solution)/shard_map/ppermute | solution.py:37
  65.3 75.7 %copy-start.5 = (f32[8,16,128]{2,1,0:T(8,128)}, f32[8,16,128]{2,1,0:T(8,128)S(1)}, u32[]{:S(2)}) copy-start(f32[8,16,128]{2,1,0:T(8,128)S(1)} %get-tuple-element.15) | copy-start | bytes 196612
  65.3 75.7 %copy-start.8 = (f32[8,16,128]{2,1,0:T(8,128)}, f32[8,16,128]{2,1,0:T(8,128)S(1)}, u32[]{:S(2)}) copy-start(f32[8,16,128]{2,1,0:T(8,128)S(1)} %get-tuple-element.16) | copy-start | bytes 196612
  65.3 75.7 %copy-start.11 = (f32[8,16,128]{2,1,0:T(8,128)}, f32[8,16,128]{2,1,0:T(8,128)S(1)}, u32[]{:S(2)}) copy-start(f32[8,16,128]{2,1,0:T(8,128)S(1)} %get-tuple-element.17) | copy-start | bytes 196612
  65.3 75.7 %copy-start.13 = (f32[8,16,128]{2,1,0:T(8,128)}, f32[8,16,128]{2,1,0:T(8,128)S(1)}, u32[]{:S(2)}) copy-start(f32[8,16,128]{2,1,0:T(8,128)S(1)} %get-tuple-element.18) | copy-start | bytes 196612
  65.3 75.7 %copy-start.15 = (f32[8,16,128]{2,1,0:T(8,128)}, f32[8,16,128]{2,1,0:T(8,128)S(1)}, u32[]{:S(2)}) copy-start(f32[8,16,128]{2,1,0:T(8,128)S(1)} %get-tuple-element.19) | copy-start | bytes 196612
  65.3 75.7 %copy-start.17 = (f32[8,16,128]{2,1,0:T(8,128)}, f32[8,16,128]{2,1,0:T(8,128)S(1)}, u32[]{:S(2)}) copy-start(f32[8,16,128]{2,1,0:T(8,128)S(1)} %get-tuple-element.20) | copy-start | bytes 196612
  65.4 5.9 %collective-permute-start.12 = (f32[1,16,128]{2,1,0:T(8,128)S(1)}, f32[1,16,128]{2,1,0:T(8,128)S(1)}, u32[]{:S(2)}, u32[]{:S(2)}) collective-permute-start(f32[1,16,128]{2,1,0:T(8,128)S(1)} %get-tuple-element.105), channel_id=1, source_target_pairs={{4,0},{8,4},{12,8},{5,1},{9,5},{13,9},{6,2},{10,6},{14,10},{7,3},{... | collective-permute-start | bytes 24584 | tf_op jit(solution)/shard_map/ppermute | solution.py:37
  66.7 5.9 %collective-permute-start.13 = (f32[1,16,128]{2,1,0:T(8,128)S(1)}, f32[1,16,128]{2,1,0:T(8,128)S(1)}, u32[]{:S(2)}, u32[]{:S(2)}) collective-permute-start(f32[1,16,128]{2,1,0:T(8,128)S(1)} %get-tuple-element.104), channel_id=1, source_target_pairs={{0,4},{4,8},{8,12},{1,5},{5,9},{9,13},{2,6},{6,10},{10,14},{3,7},{... | collective-permute-start | bytes 24584 | tf_op jit(solution)/shard_map/ppermute | solution.py:36
  72.6 4.3 %collective-permute-start.14 = (f32[10,1,128]{2,1,0:T(1,128)S(1)}, f32[10,1,128]{2,1,0:T(1,128)S(1)}, u32[]{:S(2)}, u32[]{:S(2)}) collective-permute-start(f32[10,1,128]{2,1,0:T(1,128)S(1)} %get-tuple-element.93), channel_id=1, source_target_pairs={{2,0},{3,1},{6,4},{7,5},{10,8},{11,9},{14,12},{15,13},{18,16},{19,... | collective-permute-start | bytes 15368 | tf_op jit(solution)/shard_map/ppermute | solution.py:37
  73.9 3.8 %collective-permute-start.15 = (f32[10,1,128]{2,1,0:T(1,128)S(1)}, f32[10,1,128]{2,1,0:T(1,128)S(1)}, u32[]{:S(2)}, u32[]{:S(2)}) collective-permute-start(f32[10,1,128]{2,1,0:T(1,128)S(1)} %get-tuple-element.92), channel_id=1, source_target_pairs={{0,2},{1,3},{4,6},{5,7},{8,10},{9,11},{12,14},{13,15},{16,18},{17,... | collective-permute-start | bytes 15368 | tf_op jit(solution)/shard_map/ppermute | solution.py:36
  77.9 7.5 %collective-permute-start.16 = (f32[10,18,1]{2,1,0:T(8,128)S(1)}, f32[10,18,1]{2,1,0:T(8,128)S(1)}, u32[]{:S(2)}, u32[]{:S(2)}) collective-permute-start(f32[10,18,1]{2,1,0:T(8,128)S(1)} %get-tuple-element.59), channel_id=1, source_target_pairs={{1,0},{3,2},{5,4},{7,6},{9,8},{11,10},{13,12},{15,14},{17,16},{19,... | collective-permute-start | bytes 2168 | tf_op jit(solution)/shard_map/ppermute | solution.py:37
  79.2 7.3 %collective-permute-start.17 = (f32[10,18,1]{2,1,0:T(8,128)S(1)}, f32[10,18,1]{2,1,0:T(8,128)S(1)}, u32[]{:S(2)}, u32[]{:S(2)}) collective-permute-start(f32[10,18,1]{2,1,0:T(8,128)S(1)} %get-tuple-element.58), channel_id=1, source_target_pairs={{0,1},{2,3},{4,5},{6,7},{8,9},{10,11},{12,13},{14,15},{16,17},{18,... | collective-permute-start | bytes 2168 | tf_op jit(solution)/shard_map/ppermute | solution.py:36
  87.0 6.3 %collective-permute-start.18 = (f32[1,16,128]{2,1,0:T(8,128)S(1)}, f32[1,16,128]{2,1,0:T(8,128)S(1)}, u32[]{:S(2)}, u32[]{:S(2)}) collective-permute-start(f32[1,16,128]{2,1,0:T(8,128)S(1)} %get-tuple-element.103), channel_id=1, source_target_pairs={{4,0},{8,4},{12,8},{5,1},{9,5},{13,9},{6,2},{10,6},{14,10},{7,3},{... | collective-permute-start | bytes 24584 | tf_op jit(solution)/shard_map/ppermute | solution.py:37
  88.4 6.2 %collective-permute-start.19 = (f32[1,16,128]{2,1,0:T(8,128)S(1)}, f32[1,16,128]{2,1,0:T(8,128)S(1)}, u32[]{:S(2)}, u32[]{:S(2)}) collective-permute-start(f32[1,16,128]{2,1,0:T(8,128)S(1)} %get-tuple-element.102), channel_id=1, source_target_pairs={{0,4},{4,8},{8,12},{1,5},{5,9},{9,13},{2,6},{6,10},{10,14},{3,7},{... | collective-permute-start | bytes 24584 | tf_op jit(solution)/shard_map/ppermute | solution.py:36
  94.6 4.3 %collective-permute-start.20 = (f32[10,1,128]{2,1,0:T(1,128)S(1)}, f32[10,1,128]{2,1,0:T(1,128)S(1)}, u32[]{:S(2)}, u32[]{:S(2)}) collective-permute-start(f32[10,1,128]{2,1,0:T(1,128)S(1)} %get-tuple-element.89), channel_id=1, source_target_pairs={{2,0},{3,1},{6,4},{7,5},{10,8},{11,9},{14,12},{15,13},{18,16},{19,... | collective-permute-start | bytes 15368 | tf_op jit(solution)/shard_map/ppermute | solution.py:37
  95.9 3.8 %collective-permute-start.21 = (f32[10,1,128]{2,1,0:T(1,128)S(1)}, f32[10,1,128]{2,1,0:T(1,128)S(1)}, u32[]{:S(2)}, u32[]{:S(2)}) collective-permute-start(f32[10,1,128]{2,1,0:T(1,128)S(1)} %get-tuple-element.88), channel_id=1, source_target_pairs={{0,2},{1,3},{4,6},{5,7},{8,10},{9,11},{12,14},{13,15},{16,18},{17,... | collective-permute-start | bytes 15368 | tf_op jit(solution)/shard_map/ppermute | solution.py:36
  99.9 7.6 %collective-permute-start.22 = (f32[10,18,1]{2,1,0:T(8,128)S(1)}, f32[10,18,1]{2,1,0:T(8,128)S(1)}, u32[]{:S(2)}, u32[]{:S(2)}) collective-permute-start(f32[10,18,1]{2,1,0:T(8,128)S(1)} %get-tuple-element.57), channel_id=1, source_target_pairs={{1,0},{3,2},{5,4},{7,6},{9,8},{11,10},{13,12},{15,14},{17,16},{19,... | collective-permute-start | bytes 2168 | tf_op jit(solution)/shard_map/ppermute | solution.py:37
  101.2 7.5 %collective-permute-start.23 = (f32[10,18,1]{2,1,0:T(8,128)S(1)}, f32[10,18,1]{2,1,0:T(8,128)S(1)}, u32[]{:S(2)}, u32[]{:S(2)}) collective-permute-start(f32[10,18,1]{2,1,0:T(8,128)S(1)} %get-tuple-element.56), channel_id=1, source_target_pairs={{0,1},{2,3},{4,5},{6,7},{8,9},{10,11},{12,13},{14,15},{16,17},{18,... | collective-permute-start | bytes 2168 | tf_op jit(solution)/shard_map/ppermute | solution.py:36
  110.2 6.1 %collective-permute-start.24 = (f32[1,16,128]{2,1,0:T(8,128)S(1)}, f32[1,16,128]{2,1,0:T(8,128)S(1)}, u32[]{:S(2)}, u32[]{:S(2)}) collective-permute-start(f32[1,16,128]{2,1,0:T(8,128)S(1)} %get-tuple-element.101), channel_id=1, source_target_pairs={{4,0},{8,4},{12,8},{5,1},{9,5},{13,9},{6,2},{10,6},{14,10},{7,3},{... | collective-permute-start | bytes 24584 | tf_op jit(solution)/shard_map/ppermute | solution.py:37
  111.5 6.2 %collective-permute-start.25 = (f32[1,16,128]{2,1,0:T(8,128)S(1)}, f32[1,16,128]{2,1,0:T(8,128)S(1)}, u32[]{:S(2)}, u32[]{:S(2)}) collective-permute-start(f32[1,16,128]{2,1,0:T(8,128)S(1)} %get-tuple-element.100), channel_id=1, source_target_pairs={{0,4},{4,8},{8,12},{1,5},{5,9},{9,13},{2,6},{6,10},{10,14},{3,7},{... | collective-permute-start | bytes 24584 | tf_op jit(solution)/shard_map/ppermute | solution.py:36
  117.7 6.4 %collective-permute-start.26 = (f32[10,1,128]{2,1,0:T(1,128)S(1)}, f32[10,1,128]{2,1,0:T(1,128)S(1)}, u32[]{:S(2)}, u32[]{:S(2)}) collective-permute-start(f32[10,1,128]{2,1,0:T(1,128)S(1)} %get-tuple-element.85), channel_id=1, source_target_pairs={{2,0},{3,1},{6,4},{7,5},{10,8},{11,9},{14,12},{15,13},{18,16},{19,... | collective-permute-start | bytes 15368 | tf_op jit(solution)/shard_map/ppermute | solution.py:37
  119.0 5.1 %collective-permute-start.27 = (f32[10,1,128]{2,1,0:T(1,128)S(1)}, f32[10,1,128]{2,1,0:T(1,128)S(1)}, u32[]{:S(2)}, u32[]{:S(2)}) collective-permute-start(f32[10,1,128]{2,1,0:T(1,128)S(1)} %get-tuple-element.84), channel_id=1, source_target_pairs={{0,2},{1,3},{4,6},{5,7},{8,10},{9,11},{12,14},{13,15},{16,18},{17,... | collective-permute-start | bytes 15368 | tf_op jit(solution)/shard_map/ppermute | solution.py:36
  124.3 6.8 %collective-permute-start.28 = (f32[10,18,1]{2,1,0:T(8,128)S(1)}, f32[10,18,1]{2,1,0:T(8,128)S(1)}, u32[]{:S(2)}, u32[]{:S(2)}) collective-permute-start(f32[10,18,1]{2,1,0:T(8,128)S(1)} %get-tuple-element.55), channel_id=1, source_target_pairs={{1,0},{3,2},{5,4},{7,6},{9,8},{11,10},{13,12},{15,14},{17,16},{19,... | collective-permute-start | bytes 2168 | tf_op jit(solution)/shard_map/ppermute | solution.py:37
  125.6 7.0 %collective-permute-start.29 = (f32[10,18,1]{2,1,0:T(8,128)S(1)}, f32[10,18,1]{2,1,0:T(8,128)S(1)}, u32[]{:S(2)}, u32[]{:S(2)}) collective-permute-start(f32[10,18,1]{2,1,0:T(8,128)S(1)} %get-tuple-element.54), channel_id=1, source_target_pairs={{0,1},{2,3},{4,5},{6,7},{8,9},{10,11},{12,13},{14,15},{16,17},{18,... | collective-permute-start | bytes 2168 | tf_op jit(solution)/shard_map/ppermute | solution.py:36
  134.9 7.1 %collective-permute-start.30 = (f32[1,16,128]{2,1,0:T(8,128)S(1)}, f32[1,16,128]{2,1,0:T(8,128)S(1)}, u32[]{:S(2)}, u32[]{:S(2)}) collective-permute-start(f32[1,16,128]{2,1,0:T(8,128)S(1)} %get-tuple-element.99), channel_id=1, source_target_pairs={{4,0},{8,4},{12,8},{5,1},{9,5},{13,9},{6,2},{10,6},{14,10},{7,3},{... | collective-permute-start | bytes 24584 | tf_op jit(solution)/shard_map/ppermute | solution.py:37
  136.2 6.2 %collective-permute-start.31 = (f32[1,16,128]{2,1,0:T(8,128)S(1)}, f32[1,16,128]{2,1,0:T(8,128)S(1)}, u32[]{:S(2)}, u32[]{:S(2)}) collective-permute-start(f32[1,16,128]{2,1,0:T(8,128)S(1)} %get-tuple-element.98), channel_id=1, source_target_pairs={{0,4},{4,8},{8,12},{1,5},{5,9},{9,13},{2,6},{6,10},{10,14},{3,7},{... | collective-permute-start | bytes 24584 | tf_op jit(solution)/shard_map/ppermute | solution.py:36
  143.2 5.6 %collective-permute-start.32 = (f32[10,1,128]{2,1,0:T(1,128)S(1)}, f32[10,1,128]{2,1,0:T(1,128)S(1)}, u32[]{:S(2)}, u32[]{:S(2)}) collective-permute-start(f32[10,1,128]{2,1,0:T(1,128)S(1)} %get-tuple-element.81), channel_id=1, source_target_pairs={{2,0},{3,1},{6,4},{7,5},{10,8},{11,9},{14,12},{15,13},{18,16},{19,... | collective-permute-start | bytes 15368 | tf_op jit(solution)/shard_map/ppermute | solution.py:37
  144.8 4.1 %collective-permute-start.33 = (f32[10,1,128]{2,1,0:T(1,128)S(1)}, f32[10,1,128]{2,1,0:T(1,128)S(1)}, u32[]{:S(2)}, u32[]{:S(2)}) collective-permute-start(f32[10,1,128]{2,1,0:T(1,128)S(1)} %get-tuple-element.80), channel_id=1, source_target_pairs={{0,2},{1,3},{4,6},{5,7},{8,10},{9,11},{12,14},{13,15},{16,18},{17,... | collective-permute-start | bytes 15368 | tf_op jit(solution)/shard_map/ppermute | solution.py:36
  149.7 7.3 %collective-permute-start.34 = (f32[10,18,1]{2,1,0:T(8,128)S(1)}, f32[10,18,1]{2,1,0:T(8,128)S(1)}, u32[]{:S(2)}, u32[]{:S(2)}) collective-permute-start(f32[10,18,1]{2,1,0:T(8,128)S(1)} %get-tuple-element.53), channel_id=1, source_target_pairs={{1,0},{3,2},{5,4},{7,6},{9,8},{11,10},{13,12},{15,14},{17,16},{19,... | collective-permute-start | bytes 2168 | tf_op jit(solution)/shard_map/ppermute | solution.py:37
  151.0 7.2 %collective-permute-start.35 = (f32[10,18,1]{2,1,0:T(8,128)S(1)}, f32[10,18,1]{2,1,0:T(8,128)S(1)}, u32[]{:S(2)}, u32[]{:S(2)}) collective-permute-start(f32[10,18,1]{2,1,0:T(8,128)S(1)} %get-tuple-element.52), channel_id=1, source_target_pairs={{0,1},{2,3},{4,5},{6,7},{8,9},{10,11},{12,13},{14,15},{16,17},{18,... | collective-permute-start | bytes 2168 | tf_op jit(solution)/shard_map/ppermute | solution.py:36
  162.1 8.7 %collective-permute-start.36 = (f32[1,16,128]{2,1,0:T(8,128)S(1)}, f32[1,16,128]{2,1,0:T(8,128)S(1)}, u32[]{:S(2)}, u32[]{:S(2)}) collective-permute-start(f32[1,16,128]{2,1,0:T(8,128)S(1)} %get-tuple-element.97), channel_id=1, source_target_pairs={{4,0},{8,4},{12,8},{5,1},{9,5},{13,9},{6,2},{10,6},{14,10},{7,3},{... | collective-permute-start | bytes 24584 | tf_op jit(solution)/shard_map/ppermute | solution.py:37
  163.4 7.4 %collective-permute-start.37 = (f32[1,16,128]{2,1,0:T(8,128)S(1)}, f32[1,16,128]{2,1,0:T(8,128)S(1)}, u32[]{:S(2)}, u32[]{:S(2)}) collective-permute-start(f32[1,16,128]{2,1,0:T(8,128)S(1)} %get-tuple-element.96), channel_id=1, source_target_pairs={{0,4},{4,8},{8,12},{1,5},{5,9},{9,13},{2,6},{6,10},{10,14},{3,7},{... | collective-permute-start | bytes 24584 | tf_op jit(solution)/shard_map/ppermute | solution.py:36
  171.4 6.4 %collective-permute-start.38 = (f32[10,1,128]{2,1,0:T(1,128)S(1)}, f32[10,1,128]{2,1,0:T(1,128)S(1)}, u32[]{:S(2)}, u32[]{:S(2)}) collective-permute-start(f32[10,1,128]{2,1,0:T(1,128)S(1)} %get-tuple-element.77), channel_id=1, source_target_pairs={{2,0},{3,1},{6,4},{7,5},{10,8},{11,9},{14,12},{15,13},{18,16},{19,... | collective-permute-start | bytes 15368 | tf_op jit(solution)/shard_map/ppermute | solution.py:37
  172.8 5.0 %collective-permute-start.39 = (f32[10,1,128]{2,1,0:T(1,128)S(1)}, f32[10,1,128]{2,1,0:T(1,128)S(1)}, u32[]{:S(2)}, u32[]{:S(2)}) collective-permute-start(f32[10,1,128]{2,1,0:T(1,128)S(1)} %get-tuple-element.76), channel_id=1, source_target_pairs={{0,2},{1,3},{4,6},{5,7},{8,10},{9,11},{12,14},{13,15},{16,18},{17,... | collective-permute-start | bytes 15368 | tf_op jit(solution)/shard_map/ppermute | solution.py:36
  178.9 6.8 %collective-permute-start.40 = (f32[10,18,1]{2,1,0:T(8,128)S(1)}, f32[10,18,1]{2,1,0:T(8,128)S(1)}, u32[]{:S(2)}, u32[]{:S(2)}) collective-permute-start(f32[10,18,1]{2,1,0:T(8,128)S(1)} %get-tuple-element.51), channel_id=1, source_target_pairs={{1,0},{3,2},{5,4},{7,6},{9,8},{11,10},{13,12},{15,14},{17,16},{19,... | collective-permute-start | bytes 2168 | tf_op jit(solution)/shard_map/ppermute | solution.py:37
  180.2 7.0 %collective-permute-start.41 = (f32[10,18,1]{2,1,0:T(8,128)S(1)}, f32[10,18,1]{2,1,0:T(8,128)S(1)}, u32[]{:S(2)}, u32[]{:S(2)}) collective-permute-start(f32[10,18,1]{2,1,0:T(8,128)S(1)} %get-tuple-element.50), channel_id=1, source_target_pairs={{0,1},{2,3},{4,5},{6,7},{8,9},{10,11},{12,13},{14,15},{16,17},{18,... | collective-permute-start | bytes 2168 | tf_op jit(solution)/shard_map/ppermute | solution.py:36
  (125 other events, 2150.7 us)
